TPU v7x, 32 devices: a whole 2x2x4 slice. The times are simulated.
32 devices in a mesh: req: 2 (over y), ctx: 16 (over z, x, core).
Axes of the slice: x: 2, y: 2, z: 4, core: 2. Of those that a mesh axis runs over, the one named last changes fastest.
Arguments:
- query_source: bfloat16 [2304, 256], P(('req', 'ctx')), parts along dimension 0, may hold values from -32 to 32
- key_source: bfloat16 [2304, 256], P(('req', 'ctx')), parts along dimension 0, may hold values from -4 to 4
- query_edit: bfloat16 [2304, 256], P(('req', 'ctx')), parts along dimension 0, may hold values from -32 to 32
- key_edit: bfloat16 [2304, 256], P(('req', 'ctx')), parts along dimension 0, may hold values from -4 to 4
- text_count: int32 [2], P('req'), parts along dimension 0, may hold values from 72 to 288, as said below
Outputs:
- query_grad: float32 [2304, 256], P(('req', 'ctx')), parts along dimension 0
- key_grad: float32 [2304, 256], P(('req', 'ctx')), parts along dimension 0
There are 2 independent parts, one for each index of `req`. A program takes and returns all parts, laid end to end along the dimension named above; each array names one. Nothing has to cross between parts.
Inputs may be any that keep to these rules, and one draw needn't show every extreme that they name: The first 288 positions are text slots; those at or past text_count are padding.
All inputs are finite; a program needn't handle non-finite values.
Results may differ from a plain program's by a relative error of at most 0.0095.
Values may be sent and summed in bfloat16 or wider, within the bound.
A program may use at most 64 MiB of HBM per device.

v0:
```python
import functools
import math

import jax
import jax.numpy as jnp
from jax import lax
from jax.experimental import pallas as pl
from jax.experimental.pallas import tpu as pltpu
from jax.sharding import PartitionSpec as P

HEAD_DIM = 128
MASKED = -1e30
SQUARE = True
F32 = jnp.float32
BF16 = jnp.bfloat16


def kernel(
    chips,
    count_hbm, qs_hbm, ks_hbm, qe_hbm, ke_hbm,
    qg_ref, kg_ref,
    count_ref, krecv, kother, qrecv, qother, e_buf, s_buf, piece_stats, st_send, st_recv,
    kg_send, kg_recv, qg_send, qg_recv, qg_own,
    load_sem, ksend_sem, krecv_sem, qsend_sem, qrecv_sem, st_sems,
    kgsend_sem, kgrecv_sem, qgsend_sem, qgrecv_sem,
):
    members = chips // 2
    rows = krecv.shape[3]
    all_rows = rows * chips * 2
    text_slots = min(512, all_rows // 4)
    scale = 1.0 / math.sqrt(HEAD_DIM)
    weight = 4.0 * all_rows * math.sqrt(all_rows)
    me = lax.axis_index("ctx")
    chip, core = me // 2, me % 2
    other = 1 - core

    if SQUARE:
        group, member = chip // members, chip % members
        chip_of = lambda g, m: g * members + m
    else:
        group, member = chip % 2, chip // 2
        chip_of = lambda g, m: m * 2 + g

    def dev(g, m, c):
        return {"ctx": chip_of(g, m) * 2 + c}

    def shifted(d):
        if members % 2:
            return (member + d) % members
        return (member // 2 + d // 2) % (members // 2) * 2 + (member + d) % 2

    def cycled(d):
        return (member + d) % members

    def sender(d):
        if members % 2:
            return (member + members - d) % members
        return (member // 2 + members - d // 2) % (members // 2) * 2 + (member + d) % 2

    def each(n, body, init):
        if n <= 8:
            for i in range(n):
                init = body(i, init)
            return init
        return lax.fori_loop(0, n, body, init)

    own_cols = pl.ds(pl.multiple_of(core * HEAD_DIM, HEAD_DIM), HEAD_DIM)
    other_cols = pl.ds(pl.multiple_of(other * HEAD_DIM, HEAD_DIM), HEAD_DIM)
    loads = []
    for i, (src, dst_own, dst_other) in enumerate((
        (ks_hbm, krecv.at[member, core, 0], kother.at[0]),
        (ke_hbm, krecv.at[member, core, 1], kother.at[1]),
        (qs_hbm, qrecv.at[group, core, 0], qother.at[0]),
        (qe_hbm, qrecv.at[group, core, 1], qother.at[1]),
    )):
        loads.append(pltpu.make_async_copy(src.at[:, own_cols], dst_own, load_sem.at[2 * i]))
        loads.append(pltpu.make_async_copy(src.at[:, other_cols], dst_other, load_sem.at[2 * i + 1]))
    loads.append(pltpu.make_async_copy(count_hbm, count_ref, load_sem.at[8]))
    for load in loads:
        load.start()

    barrier = pltpu.get_barrier_semaphore()

    def greet(d, carry):
        for c in (0, 1):
            pl.semaphore_signal(barrier, inc=1, device_id=dev(group, shifted(d + 1), c))
        return carry

    for c in (0, 1):
        pl.semaphore_signal(barrier, inc=1, device_id=dev(1 - group, member, c))
    pl.semaphore_signal(barrier, inc=1, device_id=dev(group, member, other))
    each(members - 1, greet, 0)
    pl.semaphore_wait(barrier, 2 * members + 1)
    for load in loads:
        load.wait()

    def key_copy(m, c, same):
        return pltpu.make_async_remote_copy(
            src_ref=krecv.at[member, core] if same else kother,
            dst_ref=krecv.at[member, core],
            send_sem=ksend_sem.at[m, c],
            recv_sem=krecv_sem.at[member, core],
            device_id=dev(group, m, c),
        )

    def key_arrival(m, c):
        return pltpu.make_async_remote_copy(
            src_ref=kother,
            dst_ref=krecv.at[m, c],
            send_sem=ksend_sem.at[m, c],
            recv_sem=krecv_sem.at[m, c],
            device_id=dev(group, m, c),
        )

    def query_copy(g, c, same):
        return pltpu.make_async_remote_copy(
            src_ref=qrecv.at[group, core] if same else qother,
            dst_ref=qrecv.at[group, core],
            send_sem=qsend_sem.at[g, c],
            recv_sem=qrecv_sem.at[group, core],
            device_id=dev(g, member, c),
        )

    def query_arrival(g, c):
        return pltpu.make_async_remote_copy(
            src_ref=qother,
            dst_ref=qrecv.at[g, c],
            send_sem=qsend_sem.at[g, c],
            recv_sem=qrecv_sem.at[g, c],
            device_id=dev(g, member, c),
        )

    query_copy(1 - group, core, True).start()
    query_copy(1 - group, other, False).start()
    query_copy(group, other, False).start()
    key_copy(member, other, False).start()

    def send_keys(d, carry):
        m = cycled(d + 1)
        key_copy(m, core, True).start()
        key_copy(m, other, False).start()
        return carry

    each(members - 1, send_keys, 0)

    count = count_ref[0]

    def valid(positions):
        return (positions >= text_slots) | (positions < count)

    query_arrival(group, other).wait_recv()
    query_arrival(1 - group, core).wait_recv()
    query_arrival(1 - group, other).wait_recv()

    def queries(which):
        pieces = [qrecv[g, c, which].astype(F32) for g in (0, 1) for c in (0, 1)]
        return jnp.concatenate(pieces, axis=0).astype(BF16)

    q_source, q_edit = queries(0), queries(1)
    width = 4 * rows
    lane = lax.broadcasted_iota(jnp.int32, (1, width), 1)
    piece = lane // rows
    lane_chip = jnp.where(piece < 2, chip_of(0, member), chip_of(1, member))
    row_place = (lane_chip * 2 + piece % 2) * rows + lane % rows
    row_weight = jnp.where(valid(row_place), 2.0 * weight, 0.0)

    def merge(a, b):
        me1, le1, ms1, ls1, sq1, cr1 = a
        me2, le2, ms2, ls2, sq2, cr2 = b
        m_e, m_s = jnp.maximum(me1, me2), jnp.maximum(ms1, ms2)
        fe1, fe2 = jnp.exp2(me1 - m_e), jnp.exp2(me2 - m_e)
        fs1, fs2 = jnp.exp2(ms1 - m_s), jnp.exp2(ms2 - m_s)
        return (
            m_e, le1 * fe1 + le2 * fe2,
            m_s, ls1 * fs1 + ls2 * fs2,
            sq1 * fe1 * fe1 + sq2 * fe2 * fe2,
            cr1 * fe1 * fs1 + cr2 * fe2 * fs2,
        )

    def powers(k, keys, q, key_valid, buf):
        scores = lax.dot_general(
            keys, q, (((1,), (1,)), ((), ())), preferred_element_type=F32
        ) * (scale * math.log2(math.e))
        scores = jnp.where(key_valid, scores, MASKED)
        top = jnp.max(scores, axis=0, keepdims=True)
        power = jnp.exp2(scores - top)
        buf[k] = power
        return top, power, jnp.sum(power, axis=0, keepdims=True)

    def score_piece(k, m, c):
        place = (chip_of(group, m) * 2 + c) * rows + lax.broadcasted_iota(jnp.int32, (rows, 1), 0)
        key_valid = valid(place)
        m_s, s_pow, l_s = powers(k, krecv[m, c, 0], q_source, key_valid, s_buf)
        m_e, e_pow, l_e = powers(k, krecv[m, c, 1], q_edit, key_valid, e_buf)
        sq = jnp.sum(e_pow * e_pow, axis=0, keepdims=True)
        cr = jnp.sum(e_pow * s_pow, axis=0, keepdims=True)
        for i, value in enumerate((m_e, l_e, m_s, l_s, sq, cr)):
            piece_stats[i, pl.ds(k, 1)] = value

    score_piece(0, member, core)
    key_arrival(member, other).wait_recv()
    score_piece(1, member, other)

    def far_scores(d, carry):
        m = cycled(members - 1 - d)
        for c in (core, other):
            key_arrival(m, c).wait_recv()
        for i, c in enumerate((core, other)):
            score_piece(2 * (d + 1) + i, m, c)
        return carry

    each(members - 1, far_scores, 0)
    tops_e, tops_s = piece_stats[0], piece_stats[2]
    m_e, m_s = jnp.max(tops_e, axis=0, keepdims=True), jnp.max(tops_s, axis=0, keepdims=True)
    f_e, f_s = jnp.exp2(tops_e - m_e), jnp.exp2(tops_s - m_s)
    stats = (
        m_e, jnp.sum(piece_stats[1] * f_e, axis=0, keepdims=True),
        m_s, jnp.sum(piece_stats[3] * f_s, axis=0, keepdims=True),
        jnp.sum(piece_stats[4] * (f_e * f_e), axis=0, keepdims=True),
        jnp.sum(piece_stats[5] * (f_e * f_s), axis=0, keepdims=True),
    )

    for i, value in enumerate(stats):
        st_send[i:i + 1] = value
    for i in (6, 7):
        st_send[i:i + 1] = jnp.zeros((1, width), F32)
    stat_copy = pltpu.make_async_remote_copy(
        src_ref=st_send, dst_ref=st_recv, send_sem=st_sems.at[0], recv_sem=st_sems.at[1],
        device_id=dev(1 - group, member, core),
    )
    stat_copy.start()
    stat_copy.wait_recv()
    m_e, l_e, m_s, l_s, sq, cr = merge(stats, tuple(st_recv[i:i + 1] for i in range(6)))
    inv_e, inv_s = 1.0 / l_e, 1.0 / l_s
    piece_stats[1] = jnp.exp2(tops_e - m_e) * inv_e
    piece_stats[3] = jnp.exp2(tops_s - m_s) * inv_s
    delta = row_weight * (sq * inv_e * inv_e - cr * inv_e * inv_s)

    def kg_copy(m, c):
        return pltpu.make_async_remote_copy(
            src_ref=kg_send.at[m, c], dst_ref=kg_recv.at[member, core],
            send_sem=kgsend_sem.at[m, c], recv_sem=kgrecv_sem.at[member, core],
            device_id=dev(group, m, c),
        )

    def kg_arrival(m, c):
        return pltpu.make_async_remote_copy(
            src_ref=kg_send.at[m, c], dst_ref=kg_recv.at[m, c],
            send_sem=kgsend_sem.at[m, c], recv_sem=kgrecv_sem.at[m, c],
            device_id=dev(group, m, c),
        )

    def qg_copy(g, c):
        return pltpu.make_async_remote_copy(
            src_ref=qg_send.at[g, c], dst_ref=qg_recv.at[group, core],
            send_sem=qgsend_sem.at[g, c], recv_sem=qgrecv_sem.at[group, core],
            device_id=dev(g, member, c),
        )

    def qg_arrival(g, c):
        return pltpu.make_async_remote_copy(
            src_ref=qg_send.at[g, c], dst_ref=qg_recv.at[g, c],
            send_sem=qgsend_sem.at[g, c], recv_sem=qgrecv_sem.at[g, c],
            device_id=dev(g, member, c),
        )

    def grad_chunk(d, m, q_total):
        grads, keys = [], []
        for i, c in enumerate((core, other)):
            k = 2 * d + i
            prob_e = e_buf[k] * piece_stats[1, pl.ds(k, 1)]
            prob_s = s_buf[k] * piece_stats[3, pl.ds(k, 1)]
            grads.append(prob_e * (row_weight * (prob_e - prob_s) - delta))
            keys.append(krecv[m, c, 1].astype(F32))
        grad = jnp.concatenate(grads, axis=0).astype(BF16)
        k_part = jnp.dot(grad, q_edit, preferred_element_type=F32) * scale
        q_part = lax.dot_general(
            jnp.concatenate(keys, axis=0).astype(BF16), grad,
            (((0,), (0,)), ((), ())), preferred_element_type=F32,
        )
        return k_part, q_part if q_total is None else q_total + q_part

    def far_grad(d, q_total):
        d = members - 1 - d
        m = cycled(members - d)
        k_part, q_total = grad_chunk(d, m, q_total)
        for i, c in enumerate((core, other)):
            kg_send[m, c] = k_part[i * rows:(i + 1) * rows].astype(BF16)
        return q_total

    q_total = each(members - 1, far_grad, jnp.zeros((HEAD_DIM, width), F32))
    k_part, q_total = grad_chunk(0, member, q_total)
    kg_mine = k_part[:rows]
    kg_send[member, other] = k_part[rows:].astype(BF16)

    q_rows = q_total.T * scale
    for g in (0, 1):
        for c in (0, 1):
            part = q_rows[(2 * g + c) * rows:(2 * g + c + 1) * rows]
            qg_own[g, c] = part
            qg_send[g, c] = part.astype(BF16)
    qg_copy(1 - group, core).start()
    qg_copy(1 - group, other).start()
    qg_copy(group, other).start()

    def send_kg(d, carry):
        m = cycled(members - 1 - d)
        for c in (core, other):
            kg_copy(m, c).start()
        return carry

    each(members - 1, send_kg, 0)
    kg_copy(member, other).start()

    def put(ref, mine, theirs):
        ref[:, :HEAD_DIM] = jnp.where(core == 0, mine, theirs)
        ref[:, HEAD_DIM:] = jnp.where(core == 0, theirs, mine)

    kg_arrival(member, other).wait_recv()

    def add_far(d, sums):
        mine, theirs = sums
        m = shifted(d + 1)
        kg_arrival(m, core).wait_recv()
        kg_arrival(m, other).wait_recv()
        return mine + kg_recv[m, core].astype(F32), theirs + kg_recv[m, other].astype(F32)

    sums = each(members - 1, add_far, (kg_mine, kg_recv[member, other].astype(F32)))
    put(kg_ref, *sums)

    qg_arrival(group, other).wait_recv()
    qg_arrival(1 - group, core).wait_recv()
    qg_arrival(1 - group, other).wait_recv()
    put(
        qg_ref,
        qg_own[group, core] + qg_recv[1 - group, core].astype(F32),
        qg_recv[group, other].astype(F32) + qg_recv[1 - group, other].astype(F32),
    )

    def drain(d, carry):
        m = shifted(d + 1)
        for c in (0, 1):
            key_copy(m, c, False).wait_send()
            kg_copy(m, c).wait_send()
        return carry

    each(members - 1, drain, 0)
    key_copy(member, other, False).wait_send()
    kg_copy(member, other).wait_send()
    for copy in (query_copy(1 - group, core, True), query_copy(1 - group, other, False),
                 query_copy(group, other, False), qg_copy(1 - group, core),
                 qg_copy(1 - group, other), qg_copy(group, other), stat_copy):
        copy.wait_send()


def put_out(qg_vmem, kg_vmem, qg_hbm, kg_hbm, sems):
    copies = (
        pltpu.make_async_copy(qg_vmem, qg_hbm, sems.at[0]),
        pltpu.make_async_copy(kg_vmem, kg_hbm, sems.at[1]),
    )
    for copy in copies:
        copy.start()
    for copy in copies:
        copy.wait()


def solution(mesh):
    chips = mesh.shape["ctx"] // 2
    members = chips // 2

    def local(query_source, key_source, query_edit, key_edit, text_count):
        rows, full = query_source.shape
        width = 4 * rows
        dma = pltpu.SemaphoreType.DMA
        vmem = pltpu.VMEM
        any_spec = pl.BlockSpec(memory_space=pl.ANY)
        grads = pl.pallas_call(
            functools.partial(kernel, chips),
            out_shape=(
                pltpu.VMEM((rows, full), F32),
                pltpu.VMEM((rows, full), F32),
            ),
            in_specs=[pl.BlockSpec(memory_space=pltpu.HBM)] * 5,
            out_specs=(pl.BlockSpec(memory_space=pltpu.VMEM),) * 2,
            scratch_shapes=[
                pltpu.SMEM((1,), jnp.int32),
                vmem((members, 2, 2, rows, HEAD_DIM), BF16),
                vmem((2, rows, HEAD_DIM), BF16),
                vmem((2, 2, 2, rows, HEAD_DIM), BF16),
                vmem((2, rows, HEAD_DIM), BF16),
                vmem((2 * members, rows, width), F32),
                vmem((2 * members, rows, width), F32),
                vmem((6, 2 * members, width), F32),
                vmem((8, width), F32),
                vmem((8, width), F32),
                vmem((members, 2, rows, HEAD_DIM), BF16),
                vmem((members, 2, rows, HEAD_DIM), BF16),
                vmem((2, 2, rows, HEAD_DIM), BF16),
                vmem((2, 2, rows, HEAD_DIM), BF16),
                vmem((2, 2, rows, HEAD_DIM), F32),
                dma((9,)),
                dma((members, 2)),
                dma((members, 2)),
                dma((2, 2)),
                dma((2, 2)),
                dma((2,)),
                dma((members, 2)),
                dma((members, 2)),
                dma((2, 2)),
                dma((2, 2)),
            ],
            compiler_params=pltpu.CompilerParams(collective_id=0, has_side_effects=True),
        )(text_count, query_source, key_source, query_edit, key_edit)
        return pl.pallas_call(
            put_out,
            out_shape=(pltpu.HBM((rows, full), F32),) * 2,
            in_specs=[pl.BlockSpec(memory_space=pltpu.VMEM)] * 2,
            out_specs=(pl.BlockSpec(memory_space=pltpu.HBM),) * 2,
            scratch_shapes=[dma((2,))],
        )(*(pltpu.with_memory_space_constraint(g, pltpu.VMEM) for g in grads))

    spec = P(("req", "ctx"), None)
    return jax.shard_map(
        local, mesh=mesh, in_specs=(spec,) * 4 + (P("req"),), out_specs=(spec, spec), check_vma=False
    )
```

profile of v0, /device:TPU:0, one launch (start us, length us, event | category | flops | bytes accessed | tf_op | source)
XLA Modules:
  0.0 22.4 jit_solution(11434904759424496967)
XLA Ops:
  1.3 20.4 %shard_map.68 = (f32[72,256]{1,0:T(8,128)S(1)}, f32[72,256]{1,0:T(8,128)S(1)}) custom-call(s32[1]{0:T(128)S(6)} %copy.7.count_hbm, bf16[72,256]{1,0:T(8,128)(2,1)} %qs_hbm.1, bf16[72,256]{1,0:T(8,128)(2,1)} %ks_hbm.1, bf16[72,256]{1,0:T(8,128)(2,1)} %qe_hbm.1, bf16[72,256]{1,0:T(8,128)(2,1)} %ke_hbm.1), custom_call_target="tpu_custom_call" | custom-call | tf_op jit(solution)/shard_map/pallas_call | solution.py:377
  21.7 0.7 %shard_map.69 = (f32[72,256]{1,0:T(8,128)}, f32[72,256]{1,0:T(8,128)}) custom-call(f32[72,256]{1,0:T(8,128)S(1)} %get-tuple-element.4.qg_vmem, f32[72,256]{1,0:T(8,128)S(1)} %get-tuple-element.5.kg_vmem), custom_call_target="tpu_custom_call" | custom-call | tf_op jit(solution)/shard_map/pallas_call | solution.py:414
where the time goes:
time: 22.5 us; the launch traced here: 22.4 us
  Pallas kernels  21.1 us (94%)
  between operations  1.29 us (6%)
    pallas_call x1, Pallas kernels, local(): pl.pallas_call(functools.partial(kernel, chips), out_shape=(pltpu.VMEM((r...  20.4 us
    pallas_call x1, Pallas kernels, local(): pl.pallas_call(put_out, out_shape=(pltpu.HBM((rows, full), F32),) * 2, in...  0.68 us

commit v1 on v0

v1 whole, which is shorter than its diff:
```python
import functools
import math

import jax
import jax.numpy as jnp
from jax import lax
from jax.experimental import pallas as pl
from jax.experimental.pallas import tpu as pltpu
from jax.sharding import PartitionSpec as P

HEAD_DIM = 128
MASKED = -1e30
F32 = jnp.float32
BF16 = jnp.bfloat16


def kernel(
    chips,
    count_hbm, qs_hbm, ks_hbm, qe_hbm, ke_hbm,
    qg_ref, kg_ref,
    count_ref, krecv, kother, qrecv, qother, qcat, kturn, e_buf, s_buf, stats_ref, st_send, st_recv,
    kg_send, kg_recv, qg_send, qg_recv, qg_own, kg_own,
    load_sem, ksend_sem, near_sem, krecv_sem, qrecv_sem, st_sems,
    kgsend_sem, gnear_sem, kgrecv_sem, qgrecv_sem,
):
    members = chips // 2
    rows = krecv.shape[3]
    pair_rows = 2 * rows
    width = 2 * pair_rows
    head = pair_rows // 128 * 128
    tail = pair_rows - head
    groups = pair_rows // 8
    all_rows = rows * chips * 2
    text_slots = min(512, all_rows // 4)
    scale = 1.0 / math.sqrt(HEAD_DIM)
    power_scale = scale * math.log2(math.e)
    weight = 4.0 * all_rows * math.sqrt(all_rows)
    me = lax.axis_index("ctx")
    chip, core = me // 2, me % 2
    other = 1 - core
    group, member = chip // members, chip % members

    def chip_of(g, m):
        return g * members + m

    def dev(g, m, c):
        return {"ctx": chip_of(g, m) * 2 + c}

    def shifted(d):
        if members % 2:
            return (member + d) % members
        return (member // 2 + d // 2) % (members // 2) * 2 + (member + d) % 2

    def sender(d):
        if members % 2:
            return (member + members - d) % members
        return (member // 2 + members - d // 2) % (members // 2) * 2 + (member + d) % 2

    def each(n, body, init):
        if n <= 8:
            for i in range(n):
                init = body(i, init)
            return init
        return lax.fori_loop(0, n, body, init)

    def wait(ref, sem):
        pltpu.make_async_copy(ref, ref, sem).wait()

    own_cols = pl.ds(pl.multiple_of(core * HEAD_DIM, HEAD_DIM), HEAD_DIM)
    other_cols = pl.ds(pl.multiple_of(other * HEAD_DIM, HEAD_DIM), HEAD_DIM)
    loads = []
    for i, (src, dst_own, dst_other) in enumerate((
        (qs_hbm, qrecv.at[0, core, 0], qother.at[0]),
        (qe_hbm, qrecv.at[0, core, 1], qother.at[1]),
        (ks_hbm, krecv.at[member, core, 0], kother.at[0]),
        (ke_hbm, krecv.at[member, core, 1], kother.at[1]),
    )):
        loads.append(pltpu.make_async_copy(src.at[:, own_cols], dst_own, load_sem.at[0]))
        loads.append(pltpu.make_async_copy(src.at[:, other_cols], dst_other, load_sem.at[0]))
    count_load = pltpu.make_async_copy(count_hbm, count_ref, load_sem.at[1])
    for load in loads:
        load.start()
    count_load.start()

    barrier = pltpu.get_barrier_semaphore()

    def greet(d, carry):
        for c in (0, 1):
            pl.semaphore_signal(barrier, inc=1, device_id=dev(group, shifted(d + 1), c))
        return carry

    for c in (0, 1):
        pl.semaphore_signal(barrier, inc=1, device_id=dev(1 - group, member, c))
    pl.semaphore_signal(barrier, inc=1, device_id=dev(group, member, other))
    each(members - 1, greet, 0)
    pl.semaphore_wait(barrier, 2 * members + 1)
    wait(krecv.at[0:2], load_sem.at[0])
    count_load.wait()

    def key_copy(m, c, same, sem):
        return pltpu.make_async_remote_copy(
            src_ref=krecv.at[member, core] if same else kother,
            dst_ref=krecv.at[member, core],
            send_sem=sem,
            recv_sem=krecv_sem.at[member],
            device_id=dev(group, m, c),
        )

    def query_copy(r, c, same):
        return pltpu.make_async_remote_copy(
            src_ref=qrecv.at[0, core] if same else qother,
            dst_ref=qrecv.at[r, core],
            send_sem=near_sem.at[0],
            recv_sem=qrecv_sem.at[r],
            device_id=dev(1 - group if r else group, member, c),
        )

    query_copy(1, core, True).start()
    query_copy(1, other, False).start()

    def send_keys(d, carry):
        m = shifted(members - 1 - d)
        key_copy(m, core, True, ksend_sem.at[0]).start()
        key_copy(m, other, False, ksend_sem.at[0]).start()
        return carry

    send_keys(0, 0)
    query_copy(0, other, False).start()
    key_copy(member, other, False, near_sem.at[0]).start()
    if members > 2:
        each(members - 2, lambda d, carry: send_keys(d + 1, carry), 0)

    count = count_ref[0]

    def valid(positions):
        return (positions >= text_slots) | (positions < count)

    lane = lax.broadcasted_iota(jnp.int32, (1, width), 1)
    in_tail = lane >= 2 * head
    spot = jnp.where(in_tail, lane - 2 * head, lane)
    half = jnp.where(in_tail, tail, head)
    far = spot >= half
    spot = jnp.where(far, spot - half, spot) + jnp.where(in_tail, head, 0)
    row_place = jnp.where(far, chip_of(1 - group, member), chip) * pair_rows + spot
    row_weight = jnp.where(valid(row_place), 2.0 * weight, 0.0)

    def place_queries(r):
        for which in (0, 1):
            joined = jnp.concatenate([qrecv[r, c, which].astype(F32) for c in (0, 1)], axis=0)
            joined = joined.astype(BF16)
            qcat[which, r * head:(r + 1) * head] = joined[:head]
            if tail:
                at = 2 * head + r * tail
                qcat[which, at:at + tail] = joined[head:]

    def powers(m, which, lanes, key_valid, buf):
        span = lanes.stop - lanes.start
        q = qcat[which, lanes]
        scores = jnp.concatenate([
            lax.dot_general(
                krecv[m, c, which], q, (((1,), (1,)), ((), ())), preferred_element_type=F32
            ) for c in (0, 1)
        ], axis=0)
        scores = jnp.where(key_valid, scores, MASKED).reshape(groups, 8, span)
        top = jnp.max(scores, axis=0)
        power = jnp.exp2((scores - top[None]) * power_scale)
        return top, power

    def score_chunk(d, m, lanes):
        place = chip_of(group, m) * pair_rows + lax.broadcasted_iota(jnp.int32, (pair_rows, 1), 0)
        key_valid = valid(place)
        m_s, s_pow = powers(m, 0, lanes, key_valid, s_buf)
        m_e, e_pow = powers(m, 1, lanes, key_valid, e_buf)
        s_buf[d, :, :, lanes] = s_pow
        e_buf[d, :, :, lanes] = e_pow
        for i, value in enumerate((
            m_e, jnp.sum(e_pow, axis=0), m_s, jnp.sum(s_pow, axis=0),
            jnp.sum(e_pow * e_pow, axis=0), jnp.sum(e_pow * s_pow, axis=0),
        )):
            stats_ref[i, d, :, lanes] = value

    early, late, full = slice(0, head), slice(head, width), slice(0, width)
    wait(qrecv.at[0, 0], qrecv_sem.at[0])
    wait(krecv.at[member, 0], krecv_sem.at[member])
    place_queries(0)
    ahead = 2 if members == 4 else 1
    for d in range(ahead):
        m = shifted(d) if d else member
        if d:
            wait(krecv.at[m], krecv_sem.at[m])
        if head:
            score_chunk(d, m, early)
    wait(qrecv.at[1], qrecv_sem.at[1])
    place_queries(1)
    for d in range(ahead):
        score_chunk(d, shifted(d) if d else member, late)

    def far_scores(d, carry):
        d = members - 1 - d
        m = sender(d)
        wait(krecv.at[m], krecv_sem.at[m])
        score_chunk(d, m, full)
        return carry

    each(members - ahead, far_scores, 0)

    def fold(op, value):
        return op(op(value, axis=0), axis=0, keepdims=True)

    tops_e, tops_s = stats_ref[0], stats_ref[2]
    m_e, m_s = fold(jnp.max, tops_e), fold(jnp.max, tops_s)
    f_e = jnp.exp2((tops_e - m_e) * power_scale)
    f_s = jnp.exp2((tops_s - m_s) * power_scale)
    stats = (
        m_e, fold(jnp.sum, stats_ref[1] * f_e),
        m_s, fold(jnp.sum, stats_ref[3] * f_s),
        fold(jnp.sum, stats_ref[4] * (f_e * f_e)),
        fold(jnp.sum, stats_ref[5] * (f_e * f_s)),
    )
    packed = jnp.concatenate(stats + (jnp.zeros((2, width), F32),), axis=0)
    st_send[:, :head] = packed[:, head:2 * head]
    st_send[:, head:2 * head] = packed[:, :head]
    if tail:
        st_send[:, 2 * head:] = jnp.concatenate(
            [packed[:, 2 * head + tail:], packed[:, 2 * head:2 * head + tail]], axis=1
        )
    stat_copy = pltpu.make_async_remote_copy(
        src_ref=st_send, dst_ref=st_recv, send_sem=st_sems.at[0], recv_sem=st_sems.at[1],
        device_id=dev(1 - group, member, core),
    )
    stat_copy.start()

    def turn_keys(d, carry):
        m = sender(d)
        joined = jnp.concatenate([krecv[m, c, 1].astype(F32) for c in (0, 1)], axis=0)
        kturn[d] = joined.T.astype(BF16)
        return carry

    each(members, turn_keys, 0)

    stat_copy.wait_recv()
    m_e1, l_e1, m_s1, l_s1, sq1, cr1 = stats
    m_e2, l_e2, m_s2, l_s2, sq2, cr2 = (st_recv[i:i + 1] for i in range(6))
    m_e, m_s = jnp.maximum(m_e1, m_e2), jnp.maximum(m_s1, m_s2)
    fe1, fe2 = jnp.exp2((m_e1 - m_e) * power_scale), jnp.exp2((m_e2 - m_e) * power_scale)
    fs1, fs2 = jnp.exp2((m_s1 - m_s) * power_scale), jnp.exp2((m_s2 - m_s) * power_scale)
    inv_e = 1.0 / (l_e1 * fe1 + l_e2 * fe2)
    inv_s = 1.0 / (l_s1 * fs1 + l_s2 * fs2)
    sq = sq1 * fe1 * fe1 + sq2 * fe2 * fe2
    cr = cr1 * fe1 * fs1 + cr2 * fe2 * fs2
    stats_ref[1] = f_e * (fe1 * inv_e)
    stats_ref[3] = f_s * (fs1 * inv_s)
    delta = row_weight * (sq * inv_e * inv_e - cr * inv_e * inv_s)

    def kg_copy(m, c, sem):
        return pltpu.make_async_remote_copy(
            src_ref=kg_send.at[m, c], dst_ref=kg_recv.at[member, core],
            send_sem=sem, recv_sem=kgrecv_sem.at[member],
            device_id=dev(group, m, c),
        )

    def qg_copy(r, c):
        return pltpu.make_async_remote_copy(
            src_ref=qg_send.at[r, c], dst_ref=qg_recv.at[r, core],
            send_sem=gnear_sem.at[0], recv_sem=qgrecv_sem.at[r],
            device_id=dev(1 - group if r else group, member, c),
        )

    q_edit = qcat[1]

    def grad_chunk(d, q_total):
        prob_e = e_buf[d] * stats_ref[1, d][None]
        prob_s = s_buf[d] * stats_ref[3, d][None]
        grad = prob_e * (row_weight[None] * (prob_e - prob_s) - delta[None])
        grad = grad.reshape(pair_rows, width).astype(BF16)
        k_part = jnp.dot(grad, q_edit, preferred_element_type=F32) * scale
        q_part = jnp.dot(kturn[d], grad, preferred_element_type=F32)
        return k_part, q_total + q_part

    def far_grad(d, q_total):
        d = members - 1 - d
        m = sender(d)
        k_part, q_total = grad_chunk(d, q_total)
        for c in (0, 1):
            kg_send[m, c] = k_part[c * rows:(c + 1) * rows].astype(BF16)
        for c in (core, other):
            kg_copy(m, c, kgsend_sem.at[0]).start()
        return q_total

    q_total = each(members - 1, far_grad, jnp.zeros((HEAD_DIM, width), F32))
    k_part, q_total = grad_chunk(0, q_total)
    for c in (0, 1):
        kg_own[c] = k_part[c * rows:(c + 1) * rows]
        kg_send[member, c] = k_part[c * rows:(c + 1) * rows].astype(BF16)

    q_rows = q_total.T * scale
    for r in (1, 0):
        joined = [q_rows[r * head:(r + 1) * head]]
        if tail:
            at = 2 * head + r * tail
            joined.append(q_rows[at:at + tail])
        joined = jnp.concatenate(joined, axis=0)
        for c in (0, 1):
            part = joined[c * rows:(c + 1) * rows]
            if not r:
                qg_own[c] = part
            qg_send[r, c] = part.astype(BF16)
        if r:
            qg_copy(1, core).start()
            qg_copy(1, other).start()
    qg_copy(0, other).start()
    kg_copy(member, other, gnear_sem.at[0]).start()

    def put(ref, mine, theirs):
        ref[:, own_cols] = mine
        ref[:, other_cols] = theirs

    wait(kg_recv.at[member, 0], kgrecv_sem.at[member])

    def add_far(d, sums):
        mine, theirs = sums
        m = shifted(d + 1)
        wait(kg_recv.at[m], kgrecv_sem.at[m])
        return mine + kg_recv[m, core].astype(F32), theirs + kg_recv[m, other].astype(F32)

    sums = each(members - 1, add_far, (kg_own[core], kg_recv[member, other].astype(F32)))
    put(kg_ref, *sums)

    wait(qg_recv.at[0, 0], qgrecv_sem.at[0])
    wait(qg_recv.at[1], qgrecv_sem.at[1])
    put(
        qg_ref,
        qg_own[core] + qg_recv[1, core].astype(F32),
        qg_recv[0, other].astype(F32) + qg_recv[1, other].astype(F32),
    )

    wait(krecv.at[0:members - 1], ksend_sem.at[0])
    wait(qrecv, near_sem.at[0])
    stat_copy.wait_send()
    wait(kg_send.at[0:members - 1], kgsend_sem.at[0])
    wait(qg_send, gnear_sem.at[0])


def put_out(qg_vmem, kg_vmem, qg_hbm, kg_hbm, sems):
    copies = (
        pltpu.make_async_copy(qg_vmem, qg_hbm, sems.at[0]),
        pltpu.make_async_copy(kg_vmem, kg_hbm, sems.at[1]),
    )
    for copy in copies:
        copy.start()
    for copy in copies:
        copy.wait()


def solution(mesh):
    chips = mesh.shape["ctx"] // 2
    members = chips // 2

    def local(query_source, key_source, query_edit, key_edit, text_count):
        rows, full = query_source.shape
        width = 4 * rows
        groups = 2 * rows // 8
        dma = pltpu.SemaphoreType.DMA
        vmem = pltpu.VMEM
        grads = pl.pallas_call(
            functools.partial(kernel, chips),
            out_shape=(
                pltpu.VMEM((rows, full), F32),
                pltpu.VMEM((rows, full), F32),
            ),
            in_specs=[pl.BlockSpec(memory_space=pltpu.HBM)] * 5,
            out_specs=(pl.BlockSpec(memory_space=pltpu.VMEM),) * 2,
            scratch_shapes=[
                pltpu.SMEM((1,), jnp.int32),
                vmem((members, 2, 2, rows, HEAD_DIM), BF16),
                vmem((2, rows, HEAD_DIM), BF16),
                vmem((2, 2, 2, rows, HEAD_DIM), BF16),
                vmem((2, rows, HEAD_DIM), BF16),
                vmem((2, width, HEAD_DIM), BF16),
                vmem((members, HEAD_DIM, 2 * rows), BF16),
                vmem((members, groups, 8, width), F32),
                vmem((members, groups, 8, width), F32),
                vmem((6, members, 8, width), F32),
                vmem((8, width), F32),
                vmem((8, width), F32),
                vmem((members, 2, rows, HEAD_DIM), BF16),
                vmem((members, 2, rows, HEAD_DIM), BF16),
                vmem((2, 2, rows, HEAD_DIM), BF16),
                vmem((2, 2, rows, HEAD_DIM), BF16),
                vmem((2, rows, HEAD_DIM), F32),
                vmem((2, rows, HEAD_DIM), F32),
                dma((2,)),
                dma((1,)),
                dma((1,)),
                dma((members,)),
                dma((2,)),
                dma((2,)),
                dma((1,)),
                dma((1,)),
                dma((members,)),
                dma((2,)),
            ],
            compiler_params=pltpu.CompilerParams(collective_id=0, has_side_effects=True),
        )(text_count, query_source, key_source, query_edit, key_edit)
        return pl.pallas_call(
            put_out,
            out_shape=(pltpu.HBM((rows, full), F32),) * 2,
            in_specs=[pl.BlockSpec(memory_space=pltpu.VMEM)] * 2,
            out_specs=(pl.BlockSpec(memory_space=pltpu.HBM),) * 2,
            scratch_shapes=[dma((2,))],
        )(*(pltpu.with_memory_space_constraint(g, pltpu.VMEM) for g in grads))

    spec = P(("req", "ctx"), None)
    return jax.shard_map(
        local, mesh=mesh, in_specs=(spec,) * 4 + (P("req"),), out_specs=(spec, spec), check_vma=False
    )
```

time: 22.5 us -> 21.6 us (0.960)
  Pallas kernels: 21.1 us -> 20.2 us
    pallas_call x1, Pallas kernels: 20.4 us -> 19.5 us  [local(): pl.pallas_call(functools.partial(kernel, chips), out_shape=(pltpu.VMEM((r...]
where the time goes in v1:
time: 21.6 us; the launch traced here: 21.5 us
  Pallas kernels  20.2 us (94%)
  between operations  1.29 us (6%)
    pallas_call x1, Pallas kernels, local(): pl.pallas_call(functools.partial(kernel, chips), out_shape=(pltpu.VMEM((r...  19.5 us
    pallas_call x1, Pallas kernels, local(): pl.pallas_call(put_out, out_shape=(pltpu.HBM((rows, full), F32),) * 2, in...  0.68 us

profile of v1, /device:TPU:0, one launch (start us, length us, event | category | flops | bytes accessed | tf_op | source)
XLA Modules:
  0.0 21.5 jit_solution(6645978021275987817)
XLA Ops:
  1.3 19.5 %shard_map.68 = (f32[72,256]{1,0:T(8,128)S(1)}, f32[72,256]{1,0:T(8,128)S(1)}) custom-call(s32[1]{0:T(128)S(6)} %copy.7.count_hbm, bf16[72,256]{1,0:T(8,128)(2,1)} %qs_hbm.1, bf16[72,256]{1,0:T(8,128)(2,1)} %ks_hbm.1, bf16[72,256]{1,0:T(8,128)(2,1)} %qe_hbm.1, bf16[72,256]{1,0:T(8,128)(2,1)} %ke_hbm.1), custom_call_target="tpu_custom_call" | custom-call | tf_op jit(solution)/shard_map/pallas_call | solution.py:365
  20.8 0.7 %shard_map.69 = (f32[72,256]{1,0:T(8,128)}, f32[72,256]{1,0:T(8,128)}) custom-call(f32[72,256]{1,0:T(8,128)S(1)} %get-tuple-element.4.qg_vmem, f32[72,256]{1,0:T(8,128)S(1)} %get-tuple-element.5.kg_vmem), custom_call_target="tpu_custom_call" | custom-call | tf_op jit(solution)/shard_map/pallas_call | solution.py:405

commit v2 on v1

v2 whole, which is shorter than its diff:
```python
import functools
import math

import jax
import jax.numpy as jnp
from jax import lax
from jax.experimental import pallas as pl
from jax.experimental.pallas import tpu as pltpu
from jax.sharding import PartitionSpec as P

HEAD_DIM = 128
MASKED = -1e30
F32 = jnp.float32
BF16 = jnp.bfloat16


def split(positions):
    members = 1
    while members * members * 4 <= positions:
        members *= 2
    while positions % members:
        members //= 2
    return members, positions // members


def kernel(
    positions,
    count_hbm, qs_hbm, ks_hbm, qe_hbm, ke_hbm,
    qg_ref, kg_ref,
    count_ref, krecv, kother, qrecv, qother, qcat, kturn, e_buf, s_buf, stats_ref, st_send, st_recv,
    kn_send, kn_recv, kg_part, kg_send, kg_recv, qg_send, qg_recv, qg_own,
    load_sem, far_sem, near_sem, kfar_sem, knear_sem, qrecv_sem, st_sems,
    kn_sem, knrecv_sem, kg_sems, qg_sems,
):
    q_span, k_span = split(positions)
    rows = krecv.shape[3]
    pair_rows = 2 * rows
    width = 2 * q_span * rows
    head = q_span * rows // 128 * 128
    groups = pair_rows // 8
    all_rows = rows * positions * 4
    text_slots = min(512, all_rows // 4)
    scale = 1.0 / math.sqrt(HEAD_DIM)
    power_scale = scale * math.log2(math.e)
    weight = 4.0 * all_rows * math.sqrt(all_rows)
    me = lax.axis_index("ctx")
    core, x, p = me % 2, me // 2 % 2, me // 4
    a, b = p % q_span, p // q_span

    def chip_of(b, a, x):
        return (b * q_span + a) * 2 + x

    def dev(b, a, x, c):
        return {"ctx": chip_of(b, a, x) * 2 + c}

    def flip(r):
        return 1 - x if isinstance(r, int) and r else x if isinstance(r, int) else (x + r) % 2

    def each(n, body, init):
        if n <= 8:
            for i in range(n):
                init = body(i, init)
            return init
        return lax.fori_loop(0, n, body, init)

    def far_first(span, i):
        return 1 - i % 2, span - 1 - i // 2

    def near_first(span, i):
        if span == 2:
            return ((0, 1), (1, 0), (1, 1))[i]
        return far_first(span, i)

    def wait(ref, sem):
        pltpu.make_async_copy(ref, ref, sem).wait()

    own_cols = pl.ds(pl.multiple_of(x * HEAD_DIM, HEAD_DIM), HEAD_DIM)
    other_cols = pl.ds(pl.multiple_of((1 - x) * HEAD_DIM, HEAD_DIM), HEAD_DIM)
    loads = []
    for src, dst_own, dst_other in (
        (ks_hbm, krecv.at[b, core, 0], kother.at[0]),
        (ke_hbm, krecv.at[b, core, 1], kother.at[1]),
        (qs_hbm, qrecv.at[a, 0], qother.at[0]),
        (qe_hbm, qrecv.at[a, 1], qother.at[1]),
    ):
        loads.append(pltpu.make_async_copy(src.at[:, own_cols], dst_own, load_sem.at[0]))
        loads.append(pltpu.make_async_copy(src.at[:, other_cols], dst_other, load_sem.at[0]))
    count_load = pltpu.make_async_copy(count_hbm, count_ref, load_sem.at[1])
    for load in loads:
        load.start()
    count_load.start()

    barrier = pltpu.get_barrier_semaphore()

    def greet_q(i, carry):
        r, d = far_first(q_span, i)
        pl.semaphore_signal(barrier, inc=1, device_id=dev(b, (a + d) % q_span, flip(r), core))
        return carry

    def greet_k(i, carry):
        r, d = far_first(k_span, i)
        pl.semaphore_signal(barrier, inc=1, device_id=dev((b + d) % k_span, a, flip(r), core))
        return carry

    each(2 * k_span - 2, greet_k, 0)
    each(2 * q_span - 1, greet_q, 0)
    pl.semaphore_signal(barrier, inc=1, device_id=dev(b, a, x, 1 - core))
    pl.semaphore_wait(barrier, 2 * k_span + 2 * q_span - 2)
    wait(krecv.at[0:2], load_sem.at[0])
    count_load.wait()

    def key_copy(r, d):
        return pltpu.make_async_remote_copy(
            src_ref=kother if isinstance(r, int) and r else krecv.at[b, core],
            dst_ref=krecv.at[r * k_span + b, core],
            send_sem=far_sem.at[0],
            recv_sem=kfar_sem.at[r * k_span + b],
            device_id=dev((b + d) % k_span, a, flip(r), core),
        )

    def query_copy(r, d):
        return pltpu.make_async_remote_copy(
            src_ref=qother if isinstance(r, int) and r else qrecv.at[a],
            dst_ref=qrecv.at[r * q_span + a],
            send_sem=far_sem.at[0],
            recv_sem=qrecv_sem.at[r],
            device_id=dev(b, (a + d) % q_span, flip(r), core),
        )

    def near_copy(s):
        return pltpu.make_async_remote_copy(
            src_ref=krecv.at[s, core],
            dst_ref=krecv.at[s, core],
            send_sem=near_sem.at[0],
            recv_sem=knear_sem.at[s],
            device_id=dev(b, a, x, 1 - core),
        )

    def fan_out(span, copy):
        def pair(i, carry):
            copy(1, span - 1 - i).start()
            copy(0, span - 1 - i).start()
            return carry

        each(span - 1, pair, 0)
        copy(1, 0).start()

    near_copy(b).start()
    fan_out(k_span, key_copy)
    fan_out(q_span, query_copy)

    count = count_ref[0]

    def valid(positions):
        return (positions >= text_slots) | (positions < count)

    lane = lax.broadcasted_iota(jnp.int32, (1, width), 1)
    lane_piece, lane_row = lane // rows, lane % rows
    lane_chip = chip_of(b, lane_piece % q_span, jnp.where(lane_piece < q_span, x, 1 - x))
    row_weight = jnp.where(valid((lane_chip * 2 + core) * rows + lane_row), 2.0 * weight, 0.0)

    def place_queries(r):
        at = r * q_span * rows
        for which in (0, 1):
            pieces = [qrecv[r * q_span + i, which].astype(F32) for i in range(q_span)]
            if r:
                pieces = ([qcat_tail[which]] if at > head else []) + pieces
            joined = jnp.concatenate(pieces, axis=0)
            start = head if r else 0
            stop = width if r else head
            if not r:
                qcat_tail.append(joined[head:])
            qcat[which, start:stop] = joined[:stop - start].astype(BF16)

    qcat_tail = []

    def powers(s, which, lanes, key_valid):
        q = qcat[which, lanes]
        scores = jnp.concatenate([
            lax.dot_general(
                krecv[s, c, which], q, (((1,), (1,)), ((), ())), preferred_element_type=F32
            ) for c in (0, 1)
        ], axis=0)
        scores = jnp.where(key_valid, scores, MASKED).reshape(groups, 8, lanes.stop - lanes.start)
        top = jnp.max(scores, axis=0)
        return top, jnp.exp2((scores - top[None]) * power_scale)

    def slot(r, d):
        return r * k_span + (b + d) % k_span

    def score_chunk(r, d, lanes):
        s = slot(r, d)
        place = chip_of((b + d) % k_span, a, flip(r)) * pair_rows
        key_valid = valid(place + lax.broadcasted_iota(jnp.int32, (pair_rows, 1), 0))
        m_s, s_pow = powers(s, 0, lanes, key_valid)
        m_e, e_pow = powers(s, 1, lanes, key_valid)
        s_buf[s, :, :, lanes] = s_pow
        e_buf[s, :, :, lanes] = e_pow
        for i, value in enumerate((
            m_e, jnp.sum(e_pow, axis=0), m_s, jnp.sum(s_pow, axis=0),
            jnp.sum(e_pow * e_pow, axis=0), jnp.sum(e_pow * s_pow, axis=0),
        )):
            stats_ref[i, s, :, lanes] = value

    early, late = slice(0, head), slice(head, width)

    def pass_on(i, carry):
        s = slot(*near_first(k_span, i))
        wait(krecv.at[s, core], kfar_sem.at[s])
        near_copy(s).start()
        return carry

    wait(krecv.at[b, 1 - core], knear_sem.at[b])
    each(2 * k_span - 1, pass_on, 0)
    wait(qrecv.at[0:q_span - 1], qrecv_sem.at[0])
    place_queries(0)
    if head:
        score_chunk(0, 0, early)

    def near_scores(i, carry):
        r, d = near_first(k_span, i)
        s = slot(r, d)
        wait(krecv.at[s, 1 - core], knear_sem.at[s])
        if head:
            score_chunk(r, d, early)
        return carry

    each(2 * k_span - 1, near_scores, 0)
    wait(qrecv.at[q_span:2 * q_span], qrecv_sem.at[1])
    place_queries(1)

    def late_scores(i, carry):
        score_chunk(*far_first(k_span, i), late)
        return carry

    each(2 * k_span - 1, late_scores, 0)
    score_chunk(0, 0, late)

    def fold(op, value):
        return op(op(value, axis=0), axis=0, keepdims=True)

    tops_e, tops_s = stats_ref[0], stats_ref[2]
    m_e, m_s = fold(jnp.max, tops_e), fold(jnp.max, tops_s)
    f_e = jnp.exp2((tops_e - m_e) * power_scale)
    f_s = jnp.exp2((tops_s - m_s) * power_scale)
    stats = (
        m_e, fold(jnp.sum, stats_ref[1] * f_e),
        m_s, fold(jnp.sum, stats_ref[3] * f_s),
        fold(jnp.sum, stats_ref[4] * (f_e * f_e)),
        fold(jnp.sum, stats_ref[5] * (f_e * f_s)),
    )
    for i, value in enumerate(stats):
        st_send[i:i + 1] = value
    for i in (6, 7):
        st_send[i:i + 1] = jnp.zeros((1, width), F32)

    def stat_copy(d):
        return pltpu.make_async_remote_copy(
            src_ref=st_send, dst_ref=st_recv.at[d - 1], send_sem=st_sems.at[0], recv_sem=st_sems.at[1],
            device_id=dev(b, (a + d) % q_span, x, core),
        )

    for d in range(1, q_span):
        stat_copy(d).start()
    stats_ref[1] = f_e
    stats_ref[3] = f_s

    def turn_keys(i, carry):
        joined = jnp.concatenate([krecv[i, c, 1].astype(F32) for c in (0, 1)], axis=0)
        kturn[i] = joined.T.astype(BF16)
        return carry

    each(2 * k_span, turn_keys, 0)

    wait(st_recv, st_sems.at[1])
    total = stats
    for d in range(q_span - 1):
        m_e1, l_e1, m_s1, l_s1, sq1, cr1 = total
        m_e2, l_e2, m_s2, l_s2, sq2, cr2 = (st_recv[d, i:i + 1] for i in range(6))
        m_e, m_s = jnp.maximum(m_e1, m_e2), jnp.maximum(m_s1, m_s2)
        fe1, fe2 = jnp.exp2((m_e1 - m_e) * power_scale), jnp.exp2((m_e2 - m_e) * power_scale)
        fs1, fs2 = jnp.exp2((m_s1 - m_s) * power_scale), jnp.exp2((m_s2 - m_s) * power_scale)
        total = (
            m_e, l_e1 * fe1 + l_e2 * fe2, m_s, l_s1 * fs1 + l_s2 * fs2,
            sq1 * fe1 * fe1 + sq2 * fe2 * fe2, cr1 * fe1 * fs1 + cr2 * fe2 * fs2,
        )
    m_e, l_e, m_s, l_s, sq, cr = total
    inv_e, inv_s = 1.0 / l_e, 1.0 / l_s
    to_e = jnp.exp2((stats[0] - m_e) * power_scale) * inv_e
    to_s = jnp.exp2((stats[2] - m_s) * power_scale) * inv_s
    delta = row_weight * (sq * inv_e * inv_e - cr * inv_e * inv_s)

    q_edit = qcat[1]

    def grad_chunk(s, q_total):
        prob_e = e_buf[s] * (stats_ref[1, s] * to_e)[None]
        prob_s = s_buf[s] * (stats_ref[3, s] * to_s)[None]
        grad = prob_e * (row_weight[None] * (prob_e - prob_s) - delta[None])
        grad = grad.reshape(pair_rows, width).astype(BF16)
        k_part = jnp.dot(grad, q_edit, preferred_element_type=F32) * scale
        q_part = jnp.dot(kturn[s], grad, preferred_element_type=F32)
        for c in (0, 1):
            part = k_part[c * rows:(c + 1) * rows]
            kg_part[s, c] = part
            kn_send[s, c] = part.astype(BF16)
        pltpu.make_async_remote_copy(
            src_ref=kn_send.at[s, 1 - core], dst_ref=kn_recv.at[s],
            send_sem=kn_sem.at[0], recv_sem=knrecv_sem.at[s],
            device_id=dev(b, a, x, 1 - core),
        ).start()
        return q_total + q_part

    q_total = each(
        2 * k_span - 1, lambda i, q: grad_chunk(slot(*far_first(k_span, i)), q),
        jnp.zeros((HEAD_DIM, width), F32),
    )
    q_total = grad_chunk(b, q_total)

    def kg_copy(r, d):
        return pltpu.make_async_remote_copy(
            src_ref=kg_send.at[slot(r, d)], dst_ref=kg_recv.at[r * k_span + b],
            send_sem=kg_sems.at[0], recv_sem=kg_sems.at[1],
            device_id=dev((b + d) % k_span, a, flip(r), core),
        )

    def qg_copy(r, d):
        return pltpu.make_async_remote_copy(
            src_ref=qg_send.at[r * q_span + (a + d) % q_span], dst_ref=qg_recv.at[r * q_span + a],
            send_sem=qg_sems.at[0], recv_sem=qg_sems.at[1],
            device_id=dev(b, (a + d) % q_span, flip(r), core),
        )

    q_rows = q_total.T * scale
    for i in range(2 * q_span):
        part = q_rows[i * rows:(i + 1) * rows]
        qg_send[i] = part.astype(BF16)
        if i < q_span:
            qg_own[i] = part
    fan_out(q_span, qg_copy)

    def joined_kg(s):
        wait(kn_recv.at[s], knrecv_sem.at[s])
        return kg_part[s, core] + kn_recv[s].astype(F32)

    def send_kg(i, carry):
        r, d = far_first(k_span, i)
        s = slot(r, d)
        kg_send[s] = joined_kg(s).astype(BF16)
        kg_copy(r, d).start()
        return carry

    each(2 * k_span - 1, send_kg, 0)
    kg_mine = joined_kg(b)

    def put(ref, mine, recv, span, at):
        others = [recv[(at + d) % span].astype(F32) for d in range(1, span)]
        theirs = [recv[span + i].astype(F32) for i in range(span)]
        ref[:, own_cols] = sum(others, mine)
        ref[:, other_cols] = sum(theirs[1:], theirs[0])

    wait(qg_recv.at[0:2 * q_span - 1], qg_sems.at[1])
    put(qg_ref, qg_own[a], qg_recv, q_span, a)
    wait(kg_recv.at[0:2 * k_span - 1], kg_sems.at[1])
    put(kg_ref, kg_mine, kg_recv, k_span, b)

    wait(krecv.at[0:q_span + k_span - 1], far_sem.at[0])
    wait(krecv.at[0:k_span], near_sem.at[0])
    wait(st_recv, st_sems.at[0])
    wait(kn_recv, kn_sem.at[0])
    wait(kg_send.at[0:2 * k_span - 1], kg_sems.at[0])
    wait(qg_send.at[0:2 * q_span - 1], qg_sems.at[0])


def put_out(qg_vmem, kg_vmem, qg_hbm, kg_hbm, sems):
    copies = (
        pltpu.make_async_copy(qg_vmem, qg_hbm, sems.at[0]),
        pltpu.make_async_copy(kg_vmem, kg_hbm, sems.at[1]),
    )
    for copy in copies:
        copy.start()
    for copy in copies:
        copy.wait()


def solution(mesh):
    positions = mesh.shape["ctx"] // 4
    q_span, k_span = split(positions)

    def local(query_source, key_source, query_edit, key_edit, text_count):
        rows, full = query_source.shape
        width = 2 * q_span * rows
        groups = 2 * rows // 8
        dma = pltpu.SemaphoreType.DMA
        vmem = pltpu.VMEM
        grads = pl.pallas_call(
            functools.partial(kernel, positions),
            out_shape=(
                pltpu.VMEM((rows, full), F32),
                pltpu.VMEM((rows, full), F32),
            ),
            in_specs=[pl.BlockSpec(memory_space=pltpu.HBM)] * 5,
            out_specs=(pl.BlockSpec(memory_space=pltpu.VMEM),) * 2,
            scratch_shapes=[
                pltpu.SMEM((1,), jnp.int32),
                vmem((2 * k_span, 2, 2, rows, HEAD_DIM), BF16),
                vmem((2, rows, HEAD_DIM), BF16),
                vmem((2 * q_span, 2, rows, HEAD_DIM), BF16),
                vmem((2, rows, HEAD_DIM), BF16),
                vmem((2, width, HEAD_DIM), BF16),
                vmem((2 * k_span, HEAD_DIM, 2 * rows), BF16),
                vmem((2 * k_span, groups, 8, width), F32),
                vmem((2 * k_span, groups, 8, width), F32),
                vmem((6, 2 * k_span, 8, width), F32),
                vmem((8, width), F32),
                vmem((q_span - 1, 8, width), F32),
                vmem((2 * k_span, 2, rows, HEAD_DIM), BF16),
                vmem((2 * k_span, rows, HEAD_DIM), BF16),
                vmem((2 * k_span, 2, rows, HEAD_DIM), F32),
                vmem((2 * k_span, rows, HEAD_DIM), BF16),
                vmem((2 * k_span, rows, HEAD_DIM), BF16),
                vmem((2 * q_span, rows, HEAD_DIM), BF16),
                vmem((2 * q_span, rows, HEAD_DIM), BF16),
                vmem((q_span, rows, HEAD_DIM), F32),
                dma((2,)),
                dma((1,)),
                dma((1,)),
                dma((2 * k_span,)),
                dma((2 * k_span,)),
                dma((2,)),
                dma((2,)),
                dma((1,)),
                dma((2 * k_span,)),
                dma((2,)),
                dma((2,)),
            ],
            compiler_params=pltpu.CompilerParams(collective_id=0, has_side_effects=True),
        )(text_count, query_source, key_source, query_edit, key_edit)
        return pl.pallas_call(
            put_out,
            out_shape=(pltpu.HBM((rows, full), F32),) * 2,
            in_specs=[pl.BlockSpec(memory_space=pltpu.VMEM)] * 2,
            out_specs=(pl.BlockSpec(memory_space=pltpu.HBM),) * 2,
            scratch_shapes=[dma((2,))],
        )(*(pltpu.with_memory_space_constraint(g, pltpu.VMEM) for g in grads))

    spec = P(("req", "ctx"), None)
    return jax.shard_map(
        local, mesh=mesh, in_specs=(spec,) * 4 + (P("req"),), out_specs=(spec, spec), check_vma=False
    )
```

time: 21.6 us -> 22.6 us (1.046)
  Pallas kernels: 20.2 us -> 21.2 us
    pallas_call x1, Pallas kernels: 19.5 us -> 20.5 us  [local(): pl.pallas_call(functools.partial(kernel, positions), out_shape=(pltpu.VME...]
where the time goes in v2:
time: 22.6 us; the launch traced here: 22.5 us
  Pallas kernels  21.2 us (94%)
  between operations  1.29 us (6%)
    pallas_call x1, Pallas kernels, local(): pl.pallas_call(functools.partial(kernel, positions), out_shape=(pltpu.VME...  20.5 us
    pallas_call x1, Pallas kernels, local(): pl.pallas_call(put_out, out_shape=(pltpu.HBM((rows, full), F32),) * 2, in...  0.68 us

profile of v2, /device:TPU:0, one launch (start us, length us, event | category | flops | bytes accessed | tf_op | source)
XLA Modules:
  0.0 22.5 jit_solution(6972261861027220355)
XLA Ops:
  1.3 20.5 %shard_map.68 = (f32[72,256]{1,0:T(8,128)S(1)}, f32[72,256]{1,0:T(8,128)S(1)}) custom-call(s32[1]{0:T(128)S(6)} %copy.7.count_hbm, bf16[72,256]{1,0:T(8,128)(2,1)} %qs_hbm.1, bf16[72,256]{1,0:T(8,128)(2,1)} %ks_hbm.1, bf16[72,256]{1,0:T(8,128)(2,1)} %qe_hbm.1, bf16[72,256]{1,0:T(8,128)(2,1)} %ke_hbm.1), custom_call_target="tpu_custom_call" | custom-call | tf_op jit(solution)/shard_map/pallas_call | solution.py:395
  21.8 0.7 %shard_map.69 = (f32[72,256]{1,0:T(8,128)}, f32[72,256]{1,0:T(8,128)}) custom-call(f32[72,256]{1,0:T(8,128)S(1)} %get-tuple-element.4.qg_vmem, f32[72,256]{1,0:T(8,128)S(1)} %get-tuple-element.5.kg_vmem), custom_call_target="tpu_custom_call" | custom-call | tf_op jit(solution)/shard_map/pallas_call | solution.py:438

commit v3 on v1

--- a/solution.py
+++ b/solution.py
@@ -18,13 +18,14 @@
     chips,
     count_hbm, qs_hbm, ks_hbm, qe_hbm, ke_hbm,
     qg_ref, kg_ref,
-    count_ref, krecv, kother, qrecv, qother, qcat, kturn, e_buf, s_buf, stats_ref, st_send, st_recv,
+    count_ref, krecv, kother, qrecv, qother, qcat, kturn, bias_ref, grad_buf, e_buf, s_buf, stats_ref,
+    st_send, st_recv,
     kg_send, kg_recv, qg_send, qg_recv, qg_own, kg_own,
     load_sem, ksend_sem, near_sem, krecv_sem, qrecv_sem, st_sems,
     kgsend_sem, gnear_sem, kgrecv_sem, qgrecv_sem,
 ):
     members = chips // 2
-    rows = krecv.shape[3]
+    rows = kother.shape[1]
     pair_rows = 2 * rows
     width = 2 * pair_rows
     head = pair_rows // 128 * 128
@@ -66,14 +67,20 @@
     def wait(ref, sem):
         pltpu.make_async_copy(ref, ref, sem).wait()
 
+    def keys(m, c):
+        return krecv.at[m, :, pl.ds(pl.multiple_of(c * rows, 8), rows)]
+
+    def chips_keys(m):
+        return krecv.at[m, :, 0:pair_rows]
+
     own_cols = pl.ds(pl.multiple_of(core * HEAD_DIM, HEAD_DIM), HEAD_DIM)
     other_cols = pl.ds(pl.multiple_of(other * HEAD_DIM, HEAD_DIM), HEAD_DIM)
     loads = []
     for i, (src, dst_own, dst_other) in enumerate((
         (qs_hbm, qrecv.at[0, core, 0], qother.at[0]),
         (qe_hbm, qrecv.at[0, core, 1], qother.at[1]),
-        (ks_hbm, krecv.at[member, core, 0], kother.at[0]),
-        (ke_hbm, krecv.at[member, core, 1], kother.at[1]),
+        (ks_hbm, keys(member, core).at[0], kother.at[0]),
+        (ke_hbm, keys(member, core).at[1], kother.at[1]),
     )):
         loads.append(pltpu.make_async_copy(src.at[:, own_cols], dst_own, load_sem.at[0]))
         loads.append(pltpu.make_async_copy(src.at[:, other_cols], dst_other, load_sem.at[0]))
@@ -94,13 +101,13 @@
     pl.semaphore_signal(barrier, inc=1, device_id=dev(group, member, other))
     each(members - 1, greet, 0)
     pl.semaphore_wait(barrier, 2 * members + 1)
-    wait(krecv.at[0:2], load_sem.at[0])
+    wait(chips_keys(slice(0, 2)), load_sem.at[0])
     count_load.wait()
 
     def key_copy(m, c, same, sem):
         return pltpu.make_async_remote_copy(
-            src_ref=krecv.at[member, core] if same else kother,
-            dst_ref=krecv.at[member, core],
+            src_ref=keys(member, core) if same else kother,
+            dst_ref=keys(member, core),
             send_sem=sem,
             recv_sem=krecv_sem.at[member],
             device_id=dev(group, m, c),
@@ -153,24 +160,31 @@
                 at = 2 * head + r * tail
                 qcat[which, at:at + tail] = joined[head:]
 
-    def powers(m, which, lanes, key_valid, buf):
+    def fill_bias(d, carry):
+        place = chip_of(group, sender(d)) * pair_rows
+        place += lax.broadcasted_iota(jnp.int32, (pair_rows, 128), 0)
+        bias_ref[d] = jnp.where(valid(place), 0.0, MASKED).reshape(groups, 8, 128)
+        return carry
+
+    each(members, fill_bias, 0)
+
+    def powers(d, m, which, lanes):
         span = lanes.stop - lanes.start
-        q = qcat[which, lanes]
+        scores = lax.dot_general(
+            krecv[m, which, 0:pair_rows], qcat[which, lanes], (((1,), (1,)), ((), ())),
+            preferred_element_type=F32,
+        ).reshape(groups, 8, span)
+        bias = bias_ref[d]
         scores = jnp.concatenate([
-            lax.dot_general(
-                krecv[m, c, which], q, (((1,), (1,)), ((), ())), preferred_element_type=F32
-            ) for c in (0, 1)
-        ], axis=0)
-        scores = jnp.where(key_valid, scores, MASKED).reshape(groups, 8, span)
+            scores[:, :, i:min(i + 128, span)] + bias[:, :, :min(128, span - i)]
+            for i in range(0, span, 128)
+        ], axis=2)
         top = jnp.max(scores, axis=0)
-        power = jnp.exp2((scores - top[None]) * power_scale)
-        return top, power
+        return top, jnp.exp2((scores - top[None]) * power_scale)
 
     def score_chunk(d, m, lanes):
-        place = chip_of(group, m) * pair_rows + lax.broadcasted_iota(jnp.int32, (pair_rows, 1), 0)
-        key_valid = valid(place)
-        m_s, s_pow = powers(m, 0, lanes, key_valid, s_buf)
-        m_e, e_pow = powers(m, 1, lanes, key_valid, e_buf)
+        m_s, s_pow = powers(d, m, 0, lanes)
+        m_e, e_pow = powers(d, m, 1, lanes)
         s_buf[d, :, :, lanes] = s_pow
         e_buf[d, :, :, lanes] = e_pow
         for i, value in enumerate((
@@ -181,13 +195,13 @@
 
     early, late, full = slice(0, head), slice(head, width), slice(0, width)
     wait(qrecv.at[0, 0], qrecv_sem.at[0])
-    wait(krecv.at[member, 0], krecv_sem.at[member])
+    wait(kother, krecv_sem.at[member])
     place_queries(0)
     ahead = 2 if members == 4 else 1
     for d in range(ahead):
         m = shifted(d) if d else member
         if d:
-            wait(krecv.at[m], krecv_sem.at[m])
+            wait(chips_keys(m), krecv_sem.at[m])
         if head:
             score_chunk(d, m, early)
     wait(qrecv.at[1], qrecv_sem.at[1])
@@ -198,7 +212,7 @@
     def far_scores(d, carry):
         d = members - 1 - d
         m = sender(d)
-        wait(krecv.at[m], krecv_sem.at[m])
+        wait(chips_keys(m), krecv_sem.at[m])
         score_chunk(d, m, full)
         return carry
 
@@ -232,8 +246,7 @@
 
     def turn_keys(d, carry):
         m = sender(d)
-        joined = jnp.concatenate([krecv[m, c, 1].astype(F32) for c in (0, 1)], axis=0)
-        kturn[d] = joined.T.astype(BF16)
+        kturn[d] = krecv[m, 1, 0:pair_rows].astype(F32).T.astype(BF16)
         return carry
 
     each(members, turn_keys, 0)
@@ -268,31 +281,35 @@
 
     q_edit = qcat[1]
 
-    def grad_chunk(d, q_total):
+    def grad_chunk(d):
         prob_e = e_buf[d] * stats_ref[1, d][None]
         prob_s = s_buf[d] * stats_ref[3, d][None]
         grad = prob_e * (row_weight[None] * (prob_e - prob_s) - delta[None])
         grad = grad.reshape(pair_rows, width).astype(BF16)
-        k_part = jnp.dot(grad, q_edit, preferred_element_type=F32) * scale
-        q_part = jnp.dot(kturn[d], grad, preferred_element_type=F32)
-        return k_part, q_total + q_part
-
-    def far_grad(d, q_total):
-        d = members - 1 - d
+        grad_buf[d] = grad
+        return jnp.dot(grad, q_edit, preferred_element_type=F32) * scale
+
+    def far_grad(i, carry):
+        d = (2, 3, 1)[i] if members == 4 else members - 1 - i
         m = sender(d)
-        k_part, q_total = grad_chunk(d, q_total)
+        k_part = grad_chunk(d)
         for c in (0, 1):
             kg_send[m, c] = k_part[c * rows:(c + 1) * rows].astype(BF16)
         for c in (core, other):
             kg_copy(m, c, kgsend_sem.at[0]).start()
-        return q_total
-
-    q_total = each(members - 1, far_grad, jnp.zeros((HEAD_DIM, width), F32))
-    k_part, q_total = grad_chunk(0, q_total)
+        return carry
+
+    each(members - 1, far_grad, 0)
+    k_part = grad_chunk(0)
     for c in (0, 1):
         kg_own[c] = k_part[c * rows:(c + 1) * rows]
         kg_send[member, c] = k_part[c * rows:(c + 1) * rows].astype(BF16)
 
+    q_total = each(
+        members,
+        lambda d, q: q + jnp.dot(kturn[d], grad_buf[d], preferred_element_type=F32),
+        jnp.zeros((HEAD_DIM, width), F32),
+    )
     q_rows = q_total.T * scale
     for r in (1, 0):
         joined = [q_rows[r * head:(r + 1) * head]]
@@ -334,7 +351,7 @@
         qg_recv[0, other].astype(F32) + qg_recv[1, other].astype(F32),
     )
 
-    wait(krecv.at[0:members - 1], ksend_sem.at[0])
+    wait(chips_keys(slice(0, members - 1)), ksend_sem.at[0])
     wait(qrecv, near_sem.at[0])
     stat_copy.wait_send()
     wait(kg_send.at[0:members - 1], kgsend_sem.at[0])
@@ -372,12 +389,14 @@
             out_specs=(pl.BlockSpec(memory_space=pltpu.VMEM),) * 2,
             scratch_shapes=[
                 pltpu.SMEM((1,), jnp.int32),
-                vmem((members, 2, 2, rows, HEAD_DIM), BF16),
+                vmem((members, 2, 2 * rows + 8, HEAD_DIM), BF16),
                 vmem((2, rows, HEAD_DIM), BF16),
                 vmem((2, 2, 2, rows, HEAD_DIM), BF16),
                 vmem((2, rows, HEAD_DIM), BF16),
                 vmem((2, width, HEAD_DIM), BF16),
                 vmem((members, HEAD_DIM, 2 * rows), BF16),
+                vmem((members, groups, 8, 128), F32),
+                vmem((members, 2 * rows, width), BF16),
                 vmem((members, groups, 8, width), F32),
                 vmem((members, groups, 8, width), F32),
                 vmem((6, members, 8, width), F32),

time: 21.6 us -> 21.9 us (1.014)
    pallas_call x1, Pallas kernels: 19.5 us -> 19.8 us  [local(): pl.pallas_call(functools.partial(kernel, chips), out_shape=(pltpu.VMEM((r...]
where the time goes in v3:
time: 21.9 us; the launch traced here: 21.7 us
  Pallas kernels  20.4 us (93%)
  between operations  1.29 us (6%)
    pallas_call x1, Pallas kernels, local(): pl.pallas_call(functools.partial(kernel, chips), out_shape=(pltpu.VMEM((r...  19.8 us
    pallas_call x1, Pallas kernels, local(): pl.pallas_call(put_out, out_shape=(pltpu.HBM((rows, full), F32),) * 2, in...  0.68 us

profile of v3, /device:TPU:0, one launch (start us, length us, event | category | flops | bytes accessed | tf_op | source)
XLA Modules:
  0.0 21.7 jit_solution(5946306211303176926)
XLA Ops:
  1.3 19.8 %shard_map.68 = (f32[72,256]{1,0:T(8,128)S(1)}, f32[72,256]{1,0:T(8,128)S(1)}) custom-call(s32[1]{0:T(128)S(6)} %copy.7.count_hbm, bf16[72,256]{1,0:T(8,128)(2,1)} %qs_hbm.1, bf16[72,256]{1,0:T(8,128)(2,1)} %ks_hbm.1, bf16[72,256]{1,0:T(8,128)(2,1)} %qe_hbm.1, bf16[72,256]{1,0:T(8,128)(2,1)} %ke_hbm.1), custom_call_target="tpu_custom_call" | custom-call | tf_op jit(solution)/shard_map/pallas_call | solution.py:382
  21.0 0.7 %shard_map.69 = (f32[72,256]{1,0:T(8,128)}, f32[72,256]{1,0:T(8,128)}) custom-call(f32[72,256]{1,0:T(8,128)S(1)} %get-tuple-element.4.qg_vmem, f32[72,256]{1,0:T(8,128)S(1)} %get-tuple-element.5.kg_vmem), custom_call_target="tpu_custom_call" | custom-call | tf_op jit(solution)/shard_map/pallas_call | solution.py:424

commit v4 on v3

--- a/solution.py
+++ b/solution.py
@@ -358,6 +358,416 @@
     wait(qg_send, gnear_sem.at[0])
 
 
+def line_kernel(
+    chips,
+    count_hbm, qs_hbm, ks_hbm, qe_hbm, ke_hbm,
+    qg_ref, kg_ref,
+    count_ref, krecv, kother, qrecv, qother, qcat, kturn, bias_ref, grad_buf, e_buf, s_buf, stats_ref,
+    st_send, st_recv,
+    st_side, st_turn, kg_send, kg_recv, qg_send, qg_recv, qg_own, kg_own,
+    load_sem, ksend_sem, near_sem, krecv_sem, qrecv_sem, st_sems, side_sems,
+    kgsend_sem, gnear_sem, gfar_sem, kgrecv_sem, qgrecv_sem,
+):
+    members = chips // 2
+    rows = kother.shape[1]
+    pair_rows = 2 * rows
+    head = pair_rows // 128 * 128
+    tail = pair_rows - head
+    width = qcat.shape[1]
+    blocks = {0: 0, 1: width - head, 2: width - 2 * head}
+    groups = pair_rows // 8
+    all_rows = rows * chips * 2
+    text_slots = min(512, all_rows // 4)
+    scale = 1.0 / math.sqrt(HEAD_DIM)
+    power_scale = scale * math.log2(math.e)
+    weight = 4.0 * all_rows * math.sqrt(all_rows)
+    me = lax.axis_index("ctx")
+    chip, core = me // 2, me % 2
+    other = 1 - core
+    group, member = chip // members, chip % members
+    inner = (group + member // 2) % 2 == 1
+    outer = (group + member // 2) % 2 == 0
+    target = (2 - group) * 2 + chip % 2
+
+    def chip_of(g, m):
+        return g * members + m
+
+    def dev(g, m, c):
+        return {"ctx": chip_of(g, m) * 2 + c}
+
+    def shifted(d):
+        if members % 2:
+            return (member + d) % members
+        return (member // 2 + d // 2) % (members // 2) * 2 + (member + d) % 2
+
+    def sender(d):
+        if members % 2:
+            return (member + members - d) % members
+        return (member // 2 + members - d // 2) % (members // 2) * 2 + (member + d) % 2
+
+    def each(n, body, init):
+        if n <= 8:
+            for i in range(n):
+                init = body(i, init)
+            return init
+        return lax.fori_loop(0, n, body, init)
+
+    def wait(ref, sem):
+        pltpu.make_async_copy(ref, ref, sem).wait()
+
+    def keys(m, c):
+        return krecv.at[m, :, pl.ds(pl.multiple_of(c * rows, 8), rows)]
+
+    def chips_keys(m):
+        return krecv.at[m, :, 0:pair_rows]
+
+    own_cols = pl.ds(pl.multiple_of(core * HEAD_DIM, HEAD_DIM), HEAD_DIM)
+    other_cols = pl.ds(pl.multiple_of(other * HEAD_DIM, HEAD_DIM), HEAD_DIM)
+    loads = []
+    for i, (src, dst_own, dst_other) in enumerate((
+        (qs_hbm, qrecv.at[0, core, 0], qother.at[0]),
+        (qe_hbm, qrecv.at[0, core, 1], qother.at[1]),
+        (ks_hbm, keys(member, core).at[0], kother.at[0]),
+        (ke_hbm, keys(member, core).at[1], kother.at[1]),
+    )):
+        loads.append(pltpu.make_async_copy(src.at[:, own_cols], dst_own, load_sem.at[0]))
+        loads.append(pltpu.make_async_copy(src.at[:, other_cols], dst_other, load_sem.at[0]))
+    count_load = pltpu.make_async_copy(count_hbm, count_ref, load_sem.at[1])
+    for load in loads:
+        load.start()
+    count_load.start()
+
+    barrier = pltpu.get_barrier_semaphore()
+
+    for c in (0, 1):
+        pl.semaphore_signal(barrier, inc=1, device_id=dev(1 - group, member, c))
+
+    @pl.when(inner)
+    def _():
+        for c in (0, 1):
+            pl.semaphore_signal(barrier, inc=1, device_id={"ctx": target * 2 + c})
+
+    for d in (3, 2, 1):
+        for c in (0, 1):
+            pl.semaphore_signal(barrier, inc=1, device_id=dev(group, shifted(d), c))
+    pl.semaphore_signal(barrier, inc=1, device_id=dev(group, member, other))
+    qcat[...] = jnp.zeros_like(qcat)
+    pl.semaphore_wait(barrier, jnp.where(inner, 2 * members + 3, 2 * members + 1))
+    wait(chips_keys(slice(0, 2)), load_sem.at[0])
+    count_load.wait()
+
+    def key_copy(m, c, same, sem):
+        return pltpu.make_async_remote_copy(
+            src_ref=keys(member, core) if same else kother,
+            dst_ref=keys(member, core),
+            send_sem=sem,
+            recv_sem=krecv_sem.at[member],
+            device_id=dev(group, m, c),
+        )
+
+    far_slot = jnp.where(inner, 1, 2)
+
+    def query_copy(far, c, same):
+        slot = far_slot if far else 0
+        return pltpu.make_async_remote_copy(
+            src_ref=qrecv.at[0, core] if same else qother,
+            dst_ref=qrecv.at[slot, core],
+            send_sem=near_sem.at[0],
+            recv_sem=qrecv_sem.at[slot],
+            device_id={"ctx": target * 2 + c} if far else dev(group, member, c),
+        )
+
+    def send_keys(d):
+        key_copy(shifted(d), core, True, ksend_sem.at[0]).start()
+        key_copy(shifted(d), other, False, ksend_sem.at[0]).start()
+
+    query_copy(1, core, True).start()
+    query_copy(1, other, False).start()
+    query_copy(0, other, False).start()
+    key_copy(member, other, False, near_sem.at[0]).start()
+    send_keys(3)
+    send_keys(2)
+    send_keys(1)
+
+    count = count_ref[0]
+
+    def valid(positions):
+        return (positions >= text_slots) | (positions < count)
+
+    lane = lax.broadcasted_iota(jnp.int32, (1, width), 1)
+    own_lane = lane < head
+    row_place = chip * pair_rows + lane
+    live = own_lane
+    for slot, owner in ((0, chip), (1, target), (2, chip_of(1 - group, member))):
+        there = lane >= head + slot * tail
+        there = there & (lane < head + (slot + 1) * tail)
+        row_place = jnp.where(there, owner * pair_rows + lane - slot * tail, row_place)
+        if slot:
+            at = blocks[slot]
+            ahead = (lane >= at) & (lane < at + head)
+            row_place = jnp.where(ahead, owner * pair_rows + lane - at, row_place)
+            there = (there | ahead) & inner
+        live = live | there
+    row_weight = jnp.where(live & valid(row_place), 2.0 * weight, 0.0)
+
+    @pl.when(outer)
+    def _():
+        for buf in (e_buf, s_buf):
+            buf[:, :, :, width - 2 * head:] = jnp.zeros((members, groups, 8, 2 * head), F32)
+
+    def place_queries(slot):
+        for which in (0, 1):
+            joined = jnp.concatenate([qrecv[slot, c, which].astype(F32) for c in (0, 1)], axis=0)
+            joined = joined.astype(BF16)
+            qcat[which, blocks[slot]:blocks[slot] + head] = joined[:head]
+            if tail:
+                at = head + slot * tail
+                qcat[which, at:at + tail] = joined[head:]
+
+    def fill_bias(d, carry):
+        place = chip_of(group, sender(d)) * pair_rows
+        place += lax.broadcasted_iota(jnp.int32, (pair_rows, 128), 0)
+        bias_ref[d] = jnp.where(valid(place), 0.0, MASKED).reshape(groups, 8, 128)
+        return carry
+
+    each(members, fill_bias, 0)
+
+    def powers(d, m, which, lanes):
+        span = lanes.stop - lanes.start
+        scores = lax.dot_general(
+            krecv[m, which, 0:pair_rows], qcat[which, lanes], (((1,), (1,)), ((), ())),
+            preferred_element_type=F32,
+        ).reshape(groups, 8, span)
+        bias = bias_ref[d]
+        scores = jnp.concatenate([
+            scores[:, :, i:min(i + 128, span)] + bias[:, :, :min(128, span - i)]
+            for i in range(0, span, 128)
+        ], axis=2)
+        top = jnp.max(scores, axis=0)
+        return top, jnp.exp2((scores - top[None]) * power_scale)
+
+    def score_chunk(d, m, lanes):
+        m_s, s_pow = powers(d, m, 0, lanes)
+        m_e, e_pow = powers(d, m, 1, lanes)
+        s_buf[d, :, :, lanes] = s_pow
+        e_buf[d, :, :, lanes] = e_pow
+        for i, value in enumerate((
+            m_e, jnp.sum(e_pow, axis=0), m_s, jnp.sum(s_pow, axis=0),
+            jnp.sum(e_pow * e_pow, axis=0), jnp.sum(e_pow * s_pow, axis=0),
+        )):
+            stats_ref[i, d, :, lanes] = value
+
+    own, late = slice(0, head), slice(head, width - head)
+    side, full, both = slice(width - head, width), slice(0, width), slice(0, width - 2 * head)
+
+    def keys_from(d):
+        m = sender(d)
+        wait(chips_keys(m), krecv_sem.at[m])
+        return m
+
+    wait(qrecv.at[0, 0], qrecv_sem.at[0])
+    wait(kother, krecv_sem.at[member])
+    place_queries(0)
+
+    @pl.when(outer)
+    def _():
+        score_chunk(0, member, both)
+        for d in (1, 3, 2):
+            score_chunk(d, keys_from(d), both)
+
+    @pl.when(inner)
+    def _():
+        score_chunk(0, member, own)
+        score_chunk(1, keys_from(1), own)
+        wait(qrecv.at[1], qrecv_sem.at[1])
+        place_queries(1)
+        score_chunk(0, member, side)
+        score_chunk(1, sender(1), side)
+        for d in (3, 2):
+            m = keys_from(d)
+            score_chunk(d, m, own)
+            score_chunk(d, m, side)
+        wait(qrecv.at[2], qrecv_sem.at[2])
+        place_queries(2)
+        for d in range(4):
+            score_chunk(d, sender(d) if d else member, late)
+
+    def fold(op, value):
+        return op(op(value, axis=0), axis=0, keepdims=True)
+
+    tops_e, tops_s = stats_ref[0], stats_ref[2]
+    m_e, m_s = fold(jnp.max, tops_e), fold(jnp.max, tops_s)
+    f_e = jnp.exp2((tops_e - m_e) * power_scale)
+    f_s = jnp.exp2((tops_s - m_s) * power_scale)
+    stats = (
+        m_e, fold(jnp.sum, stats_ref[1] * f_e),
+        m_s, fold(jnp.sum, stats_ref[3] * f_s),
+        fold(jnp.sum, stats_ref[4] * (f_e * f_e)),
+        fold(jnp.sum, stats_ref[5] * (f_e * f_s)),
+    )
+    packed = jnp.concatenate(stats + (jnp.zeros((2, width), F32),), axis=0)
+    span = width - 3 * head
+    tails = packed[:, head:head + span]
+    st_send[:, :head] = jnp.where(inner, packed[:, blocks[2]:blocks[2] + head], packed[:, :head])
+    st_send[:, head:] = jnp.where(
+        inner, pltpu.roll(tails, span - 2 * tail, 1), pltpu.roll(tails, 2 * tail, 1)
+    )
+    stat_copy = pltpu.make_async_remote_copy(
+        src_ref=st_send, dst_ref=st_recv, send_sem=st_sems.at[0], recv_sem=st_sems.at[1],
+        device_id=dev(1 - group, member, core),
+    )
+    stat_copy.start()
+    side_copy = pltpu.make_async_remote_copy(
+        src_ref=st_side, dst_ref=st_turn, send_sem=side_sems.at[0], recv_sem=side_sems.at[1],
+        device_id={"ctx": target * 2 + core},
+    )
+
+    @pl.when(inner)
+    def _():
+        st_side[:, :head] = packed[:, blocks[1]:]
+        st_side[:, head:2 * head] = packed[:, :head]
+        tail_lane = lax.broadcasted_iota(jnp.int32, (8, span), 1)
+        st_side[:, 2 * head:] = jnp.where(
+            tail_lane < tail, pltpu.roll(tails, span - tail, 1), pltpu.roll(tails, tail, 1)
+        )
+        side_copy.start()
+
+    def turn_keys(d, carry):
+        m = sender(d)
+        kturn[d] = krecv[m, 1, 0:pair_rows].astype(F32).T.astype(BF16)
+        return carry
+
+    each(members, turn_keys, 0)
+
+    @pl.when(inner)
+    def _():
+        side_copy.wait_recv()
+
+    stat_copy.wait_recv()
+    there, turned = st_recv[...], st_turn[...]
+    tail_lane = lax.broadcasted_iota(jnp.int32, (8, span), 1)
+    second = jnp.concatenate([
+        jnp.where(inner, turned[:, :head], there[:, :head]),
+        jnp.where(inner & (tail_lane < 2 * tail), turned[:, 2 * head:], there[:, head:]),
+        there[:, :head],
+        turned[:, head:2 * head],
+    ], axis=1)
+    m_e1, l_e1, m_s1, l_s1, sq1, cr1 = stats
+    m_e2, l_e2, m_s2, l_s2, sq2, cr2 = (second[i:i + 1] for i in range(6))
+    m_e, m_s = jnp.maximum(m_e1, m_e2), jnp.maximum(m_s1, m_s2)
+    fe1, fe2 = jnp.exp2((m_e1 - m_e) * power_scale), jnp.exp2((m_e2 - m_e) * power_scale)
+    fs1, fs2 = jnp.exp2((m_s1 - m_s) * power_scale), jnp.exp2((m_s2 - m_s) * power_scale)
+    inv_e = 1.0 / (l_e1 * fe1 + l_e2 * fe2)
+    inv_s = 1.0 / (l_s1 * fs1 + l_s2 * fs2)
+    sq = sq1 * fe1 * fe1 + sq2 * fe2 * fe2
+    cr = cr1 * fe1 * fs1 + cr2 * fe2 * fs2
+    stats_ref[1] = jnp.where(live, f_e * (fe1 * inv_e), 0.0)
+    stats_ref[3] = jnp.where(live, f_s * (fs1 * inv_s), 0.0)
+    delta = jnp.where(live, row_weight * (sq * inv_e * inv_e - cr * inv_e * inv_s), 0.0)
+
+    def kg_copy(m, c, sem):
+        return pltpu.make_async_remote_copy(
+            src_ref=kg_send.at[m, c], dst_ref=kg_recv.at[member, core],
+            send_sem=sem, recv_sem=kgrecv_sem.at[member],
+            device_id=dev(group, m, c),
+        )
+
+    def qg_copy(slot, c):
+        return pltpu.make_async_remote_copy(
+            src_ref=qg_send.at[slot, c], dst_ref=qg_recv.at[1 if slot else 0, core],
+            send_sem=gfar_sem.at[0] if slot else gnear_sem.at[0],
+            recv_sem=qgrecv_sem.at[1 if slot else 0],
+            device_id=(dev(group, member, c), {"ctx": target * 2 + c}, dev(1 - group, member, c))[slot],
+        )
+
+    q_edit = qcat[1]
+
+    def grad_chunk(d):
+        prob_e = e_buf[d] * stats_ref[1, d][None]
+        prob_s = s_buf[d] * stats_ref[3, d][None]
+        grad = prob_e * (row_weight[None] * (prob_e - prob_s) - delta[None])
+        grad = grad.reshape(pair_rows, width).astype(BF16)
+        grad_buf[d] = grad
+        return jnp.dot(grad, q_edit, preferred_element_type=F32) * scale
+
+    def far_grad(i, carry):
+        d = (2, 3, 1)[i] if members == 4 else members - 1 - i
+        m = sender(d)
+        k_part = grad_chunk(d)
+        for c in (0, 1):
+            kg_send[m, c] = k_part[c * rows:(c + 1) * rows].astype(BF16)
+        for c in (core, other):
+            kg_copy(m, c, kgsend_sem.at[0]).start()
+        return carry
+
+    each(members - 1, far_grad, 0)
+    k_part = grad_chunk(0)
+    for c in (0, 1):
+        kg_own[c] = k_part[c * rows:(c + 1) * rows]
+        kg_send[member, c] = k_part[c * rows:(c + 1) * rows].astype(BF16)
+
+    q_total = each(
+        members,
+        lambda d, q: q + jnp.dot(kturn[d], grad_buf[d], preferred_element_type=F32),
+        jnp.zeros((HEAD_DIM, width), F32),
+    )
+    q_rows = q_total.T * scale
+    for slot in (2, 1, 0):
+        joined = [q_rows[blocks[slot]:blocks[slot] + head]]
+        if tail:
+            at = head + slot * tail
+            joined.append(q_rows[at:at + tail])
+        joined = jnp.concatenate(joined, axis=0)
+        for c in (0, 1):
+            part = joined[c * rows:(c + 1) * rows]
+            if not slot:
+                qg_own[c] = part
+            qg_send[slot, c] = part.astype(BF16)
+
+    @pl.when(inner)
+    def _():
+        for slot in (2, 1):
+            qg_copy(slot, core).start()
+            qg_copy(slot, other).start()
+
+    qg_copy(0, other).start()
+    kg_copy(member, other, gnear_sem.at[0]).start()
+
+    def put(ref, mine, theirs):
+        ref[:, own_cols] = mine
+        ref[:, other_cols] = theirs
+
+    wait(kg_recv.at[member, 0], kgrecv_sem.at[member])
+
+    def add_far(d, sums):
+        mine, theirs = sums
+        m = shifted(d + 1)
+        wait(kg_recv.at[m], kgrecv_sem.at[m])
+        return mine + kg_recv[m, core].astype(F32), theirs + kg_recv[m, other].astype(F32)
+
+    sums = each(members - 1, add_far, (kg_own[core], kg_recv[member, other].astype(F32)))
+    put(kg_ref, *sums)
+
+    wait(qg_recv.at[0, 0], qgrecv_sem.at[0])
+    wait(qg_recv.at[1], qgrecv_sem.at[1])
+    put(
+        qg_ref,
+        qg_own[core] + qg_recv[1, core].astype(F32),
+        qg_recv[0, other].astype(F32) + qg_recv[1, other].astype(F32),
+    )
+
+    wait(chips_keys(slice(0, members - 1)), ksend_sem.at[0])
+    wait(qrecv.at[0:2], near_sem.at[0])
+    stat_copy.wait_send()
+    wait(kg_send.at[0:members - 1], kgsend_sem.at[0])
+    wait(qg_send.at[0], gnear_sem.at[0])
+
+    @pl.when(inner)
+    def _():
+        wait(qg_send.at[1:3], gfar_sem.at[0])
+        side_copy.wait_send()
+
+
 def put_out(qg_vmem, kg_vmem, qg_hbm, kg_hbm, sems):
     copies = (
         pltpu.make_async_copy(qg_vmem, qg_hbm, sems.at[0]),
@@ -379,8 +789,16 @@
         groups = 2 * rows // 8
         dma = pltpu.SemaphoreType.DMA
         vmem = pltpu.VMEM
+        in_line = chips == 8
+        if in_line:
+            pair = 2 * rows
+            head = pair // 128 * 128
+            width = 3 * head + -(-3 * (pair - head) // 128) * 128
+        slots = 3 if in_line else 2
+        stat = vmem((8, width - 2 * head if in_line else width), F32)
+        side = [vmem((8, width - head), F32)] * 2 if in_line else []
         grads = pl.pallas_call(
-            functools.partial(kernel, chips),
+            functools.partial(line_kernel if in_line else kernel, chips),
             out_shape=(
                 pltpu.VMEM((rows, full), F32),
                 pltpu.VMEM((rows, full), F32),
@@ -391,7 +809,7 @@
                 pltpu.SMEM((1,), jnp.int32),
                 vmem((members, 2, 2 * rows + 8, HEAD_DIM), BF16),
                 vmem((2, rows, HEAD_DIM), BF16),
-                vmem((2, 2, 2, rows, HEAD_DIM), BF16),
+                vmem((slots, 2, 2, rows, HEAD_DIM), BF16),
                 vmem((2, rows, HEAD_DIM), BF16),
                 vmem((2, width, HEAD_DIM), BF16),
                 vmem((members, HEAD_DIM, 2 * rows), BF16),
@@ -400,11 +818,12 @@
                 vmem((members, groups, 8, width), F32),
                 vmem((members, groups, 8, width), F32),
                 vmem((6, members, 8, width), F32),
-                vmem((8, width), F32),
-                vmem((8, width), F32),
+                stat,
+                stat,
+                *side,
                 vmem((members, 2, rows, HEAD_DIM), BF16),
                 vmem((members, 2, rows, HEAD_DIM), BF16),
-                vmem((2, 2, rows, HEAD_DIM), BF16),
+                vmem((slots, 2, rows, HEAD_DIM), BF16),
                 vmem((2, 2, rows, HEAD_DIM), BF16),
                 vmem((2, rows, HEAD_DIM), F32),
                 vmem((2, rows, HEAD_DIM), F32),
@@ -412,10 +831,12 @@
                 dma((1,)),
                 dma((1,)),
                 dma((members,)),
+                dma((slots,)),
                 dma((2,)),
-                dma((2,)),
+                *([dma((2,))] if in_line else []),
                 dma((1,)),
                 dma((1,)),
+                *([dma((1,))] if in_line else []),
                 dma((members,)),
                 dma((2,)),
             ],

time: 21.9 us -> 21.2 us (0.968)
  Pallas kernels: 20.4 us -> 19.7 us
    pallas_call x1, Pallas kernels: 19.8 us -> 19.1 us  [local(): pl.pallas_call(functools.partial(line_kernel if in_line else kernel, chip...]
where the time goes in v4:
time: 21.2 us; the launch traced here: 21 us
  Pallas kernels  19.7 us (93%)
  between operations  1.29 us (6%)
    pallas_call x1, Pallas kernels, local(): pl.pallas_call(functools.partial(line_kernel if in_line else kernel, chip...  19.1 us
    pallas_call x1, Pallas kernels, local(): pl.pallas_call(put_out, out_shape=(pltpu.HBM((rows, full), F32),) * 2, in...  0.68 us

profile of v4, /device:TPU:0, one launch (start us, length us, event | category | flops | bytes accessed | tf_op | source)
XLA Modules:
  0.0 21.0 jit_solution(10049939353260304559)
XLA Ops:
  1.3 19.1 %shard_map.68 = (f32[72,256]{1,0:T(8,128)S(1)}, f32[72,256]{1,0:T(8,128)S(1)}) custom-call(s32[1]{0:T(128)S(6)} %copy.7.count_hbm, bf16[72,256]{1,0:T(8,128)(2,1)} %qs_hbm.1, bf16[72,256]{1,0:T(8,128)(2,1)} %ks_hbm.1, bf16[72,256]{1,0:T(8,128)(2,1)} %qe_hbm.1, bf16[72,256]{1,0:T(8,128)(2,1)} %ke_hbm.1), custom_call_target="tpu_custom_call" | custom-call | tf_op jit(solution)/shard_map/pallas_call | solution.py:800
  20.4 0.7 %shard_map.69 = (f32[72,256]{1,0:T(8,128)}, f32[72,256]{1,0:T(8,128)}) custom-call(f32[72,256]{1,0:T(8,128)S(1)} %get-tuple-element.4.qg_vmem, f32[72,256]{1,0:T(8,128)S(1)} %get-tuple-element.5.kg_vmem), custom_call_target="tpu_custom_call" | custom-call | tf_op jit(solution)/shard_map/pallas_call | solution.py:845

commit v5 on v4

--- a/solution.py
+++ b/solution.py
@@ -421,8 +421,9 @@
     def chips_keys(m):
         return krecv.at[m, :, 0:pair_rows]
 
-    own_cols = pl.ds(pl.multiple_of(core * HEAD_DIM, HEAD_DIM), HEAD_DIM)
-    other_cols = pl.ds(pl.multiple_of(other * HEAD_DIM, HEAD_DIM), HEAD_DIM)
+    own_head = (core + group) % 2
+    own_cols = pl.ds(pl.multiple_of(own_head * HEAD_DIM, HEAD_DIM), HEAD_DIM)
+    other_cols = pl.ds(pl.multiple_of((1 - own_head) * HEAD_DIM, HEAD_DIM), HEAD_DIM)
     loads = []
     for i, (src, dst_own, dst_other) in enumerate((
         (qs_hbm, qrecv.at[0, core, 0], qother.at[0]),
@@ -481,8 +482,8 @@
         key_copy(shifted(d), core, True, ksend_sem.at[0]).start()
         key_copy(shifted(d), other, False, ksend_sem.at[0]).start()
 
-    query_copy(1, core, True).start()
-    query_copy(1, other, False).start()
+    query_copy(1, other, True).start()
+    query_copy(1, core, False).start()
     query_copy(0, other, False).start()
     key_copy(member, other, False, near_sem.at[0]).start()
     send_keys(3)
@@ -577,20 +578,16 @@
 
     @pl.when(inner)
     def _():
-        score_chunk(0, member, own)
-        score_chunk(1, keys_from(1), own)
-        wait(qrecv.at[1], qrecv_sem.at[1])
-        place_queries(1)
-        score_chunk(0, member, side)
-        score_chunk(1, sender(1), side)
+        for slot in (1, 2):
+            wait(qrecv.at[slot], qrecv_sem.at[slot])
+        for slot in (1, 2):
+            place_queries(slot)
+        score_chunk(0, member, full)
+        score_chunk(1, keys_from(1), full)
         for d in (3, 2):
-            m = keys_from(d)
-            score_chunk(d, m, own)
-            score_chunk(d, m, side)
-        wait(qrecv.at[2], qrecv_sem.at[2])
-        place_queries(2)
-        for d in range(4):
-            score_chunk(d, sender(d) if d else member, late)
+            keys_from(d)
+        for d in (3, 2):
+            score_chunk(d, sender(d), full)
 
     def fold(op, value):
         return op(op(value, axis=0), axis=0, keepdims=True)
@@ -614,12 +611,11 @@
     )
     stat_copy = pltpu.make_async_remote_copy(
         src_ref=st_send, dst_ref=st_recv, send_sem=st_sems.at[0], recv_sem=st_sems.at[1],
-        device_id=dev(1 - group, member, core),
-    )
-    stat_copy.start()
+        device_id=dev(1 - group, member, other),
+    )
     side_copy = pltpu.make_async_remote_copy(
         src_ref=st_side, dst_ref=st_turn, send_sem=side_sems.at[0], recv_sem=side_sems.at[1],
-        device_id={"ctx": target * 2 + core},
+        device_id={"ctx": target * 2 + other},
     )
 
     @pl.when(inner)
@@ -631,6 +627,8 @@
             tail_lane < tail, pltpu.roll(tails, span - tail, 1), pltpu.roll(tails, tail, 1)
         )
         side_copy.start()
+
+    stat_copy.start()
 
     def turn_keys(d, carry):
         m = sender(d)
@@ -752,8 +750,8 @@
     wait(qg_recv.at[1], qgrecv_sem.at[1])
     put(
         qg_ref,
-        qg_own[core] + qg_recv[1, core].astype(F32),
-        qg_recv[0, other].astype(F32) + qg_recv[1, other].astype(F32),
+        qg_own[core] + qg_recv[1, other].astype(F32),
+        qg_recv[0, other].astype(F32) + qg_recv[1, core].astype(F32),
     )
 
     wait(chips_keys(slice(0, members - 1)), ksend_sem.at[0])

time: 21.2 us -> 20.8 us (0.981)
  Pallas kernels: 19.7 us -> 19.4 us
    pallas_call x1, Pallas kernels: 19.1 us -> 18.7 us  [local(): pl.pallas_call(functools.partial(line_kernel if in_line else kernel, chip...]
where the time goes in v5:
time: 20.8 us; the launch traced here: 20.7 us
  Pallas kernels  19.4 us (93%)
  between operations  1.29 us (6%)
    pallas_call x1, Pallas kernels, local(): pl.pallas_call(functools.partial(line_kernel if in_line else kernel, chip...  18.7 us
    pallas_call x1, Pallas kernels, local(): pl.pallas_call(put_out, out_shape=(pltpu.HBM((rows, full), F32),) * 2, in...  0.68 us

profile of v5, /device:TPU:0, one launch (start us, length us, event | category | flops | bytes accessed | tf_op | source)
XLA Modules:
  0.0 20.7 jit_solution(18296604702617291547)
XLA Ops:
  1.3 18.7 %shard_map.68 = (f32[72,256]{1,0:T(8,128)S(1)}, f32[72,256]{1,0:T(8,128)S(1)}) custom-call(s32[1]{0:T(128)S(6)} %copy.7.count_hbm, bf16[72,256]{1,0:T(8,128)(2,1)} %qs_hbm.1, bf16[72,256]{1,0:T(8,128)(2,1)} %ks_hbm.1, bf16[72,256]{1,0:T(8,128)(2,1)} %qe_hbm.1, bf16[72,256]{1,0:T(8,128)(2,1)} %ke_hbm.1), custom_call_target="tpu_custom_call" | custom-call | tf_op jit(solution)/shard_map/pallas_call | solution.py:798
  20.0 0.7 %shard_map.69 = (f32[72,256]{1,0:T(8,128)}, f32[72,256]{1,0:T(8,128)}) custom-call(f32[72,256]{1,0:T(8,128)S(1)} %get-tuple-element.4.qg_vmem, f32[72,256]{1,0:T(8,128)S(1)} %get-tuple-element.5.kg_vmem), custom_call_target="tpu_custom_call" | custom-call | tf_op jit(solution)/shard_map/pallas_call | solution.py:843

commit v6 on v5

--- a/solution.py
+++ b/solution.py
@@ -694,7 +694,7 @@
         k_part = grad_chunk(d)
         for c in (0, 1):
             kg_send[m, c] = k_part[c * rows:(c + 1) * rows].astype(BF16)
-        for c in (core, other):
+        for c in (0, 1):
             kg_copy(m, c, kgsend_sem.at[0]).start()
         return carry
 
@@ -725,8 +725,8 @@
     @pl.when(inner)
     def _():
         for slot in (2, 1):
-            qg_copy(slot, core).start()
-            qg_copy(slot, other).start()
+            for c in (0, 1):
+                qg_copy(slot, c).start()
 
     qg_copy(0, other).start()
     kg_copy(member, other, gnear_sem.at[0]).start()

time: 20.8 us -> 20.7 us (level)
  no operation moved by 1% of the time
where the time goes in v6:
time: 20.7 us; the launch traced here: 20.6 us
  Pallas kernels  19.3 us (93%)
  between operations  1.29 us (6%)
    pallas_call x1, Pallas kernels, local(): pl.pallas_call(functools.partial(line_kernel if in_line else kernel, chip...  18.6 us
    pallas_call x1, Pallas kernels, local(): pl.pallas_call(put_out, out_shape=(pltpu.HBM((rows, full), F32),) * 2, in...  0.68 us

profile of v6, /device:TPU:0, one launch (start us, length us, event | category | flops | bytes accessed | tf_op | source)
XLA Modules:
  0.0 20.6 jit_solution(1634228850286686319)
XLA Ops:
  1.3 18.6 %shard_map.68 = (f32[72,256]{1,0:T(8,128)S(1)}, f32[72,256]{1,0:T(8,128)S(1)}) custom-call(s32[1]{0:T(128)S(6)} %copy.7.count_hbm, bf16[72,256]{1,0:T(8,128)(2,1)} %qs_hbm.1, bf16[72,256]{1,0:T(8,128)(2,1)} %ks_hbm.1, bf16[72,256]{1,0:T(8,128)(2,1)} %qe_hbm.1, bf16[72,256]{1,0:T(8,128)(2,1)} %ke_hbm.1), custom_call_target="tpu_custom_call" | custom-call | tf_op jit(solution)/shard_map/pallas_call | solution.py:798
  19.9 0.7 %shard_map.69 = (f32[72,256]{1,0:T(8,128)}, f32[72,256]{1,0:T(8,128)}) custom-call(f32[72,256]{1,0:T(8,128)S(1)} %get-tuple-element.4.qg_vmem, f32[72,256]{1,0:T(8,128)S(1)} %get-tuple-element.5.kg_vmem), custom_call_target="tpu_custom_call" | custom-call | tf_op jit(solution)/shard_map/pallas_call | solution.py:843

commit v7 on v6

--- a/solution.py
+++ b/solution.py
@@ -583,10 +583,9 @@
         for slot in (1, 2):
             place_queries(slot)
         score_chunk(0, member, full)
-        score_chunk(1, keys_from(1), full)
-        for d in (3, 2):
+        for d in (1, 2, 3):
             keys_from(d)
-        for d in (3, 2):
+        for d in (1, 2, 3):
             score_chunk(d, sender(d), full)
 
     def fold(op, value):

time: 20.7 us -> 20.8 us (level)
  no operation moved by 1% of the time
where the time goes in v7:
time: 20.8 us; the launch traced here: 20.7 us
  Pallas kernels  19.4 us (93%)
  between operations  1.29 us (6%)
    pallas_call x1, Pallas kernels, local(): pl.pallas_call(functools.partial(line_kernel if in_line else kernel, chip...  18.7 us
    pallas_call x1, Pallas kernels, local(): pl.pallas_call(put_out, out_shape=(pltpu.HBM((rows, full), F32),) * 2, in...  0.68 us

profile of v7, /device:TPU:0, one launch (start us, length us, event | category | flops | bytes accessed | tf_op | source)
XLA Modules:
  0.0 20.7 jit_solution(774902871138958433)
XLA Ops:
  1.3 18.7 %shard_map.68 = (f32[72,256]{1,0:T(8,128)S(1)}, f32[72,256]{1,0:T(8,128)S(1)}) custom-call(s32[1]{0:T(128)S(6)} %copy.7.count_hbm, bf16[72,256]{1,0:T(8,128)(2,1)} %qs_hbm.1, bf16[72,256]{1,0:T(8,128)(2,1)} %ks_hbm.1, bf16[72,256]{1,0:T(8,128)(2,1)} %qe_hbm.1, bf16[72,256]{1,0:T(8,128)(2,1)} %ke_hbm.1), custom_call_target="tpu_custom_call" | custom-call | tf_op jit(solution)/shard_map/pallas_call | solution.py:797
  20.0 0.7 %shard_map.69 = (f32[72,256]{1,0:T(8,128)}, f32[72,256]{1,0:T(8,128)}) custom-call(f32[72,256]{1,0:T(8,128)S(1)} %get-tuple-element.4.qg_vmem, f32[72,256]{1,0:T(8,128)S(1)} %get-tuple-element.5.kg_vmem), custom_call_target="tpu_custom_call" | custom-call | tf_op jit(solution)/shard_map/pallas_call | solution.py:842
